TPU v7x, 32 devices: a whole 2x2x4 slice. The times are simulated.
32 devices in a mesh: expert: 8 (over z, x), dp: 4 (over y, core).
Axes of the slice: x: 2, y: 2, z: 4, core: 2. Of those that a mesh axis runs over, the one named last changes fastest.
Arguments:
- tokens: bfloat16 [4096, 2048], P(('expert', 'dp')), may hold values from -6 to 6
- routes: int32 [4096, 8], P(('expert', 'dp')), may hold values from 0 to 63, all different within a row; in each aligned block of 128 rows (0 to 127, 128 to 255, ...) at most 32 rows name the same one
- gates: float32 [4096, 8], P(('expert', 'dp')), may hold values from 0.1 to 1
- cotangent: bfloat16 [4096, 2048], P(('expert', 'dp')), may hold values from -6 to 6
- w_up: bfloat16 [64, 2048, 128], P('expert'), may hold values from -0.125 to 0.125
- w_down: bfloat16 [64, 128, 2048], P('expert'), may hold values from -0.5 to 0.5
Outputs:
- mixed: bfloat16 [4096, 2048], P(('expert', 'dp'))
- token_grad: bfloat16 [4096, 2048], P(('expert', 'dp'))
- grad_up: bfloat16 [64, 2048, 128], P('expert', 'dp')
- grad_down: bfloat16 [64, 128, 2048], P('expert', None, 'dp')
Inputs may be any that keep to these rules, and one draw needn't show every extreme that they name: `routes`: each row names 8 different experts; within the rows of one device no expert is named more than min(32, 128) times, and some expert is named exactly that often.
All inputs are finite; a program needn't handle non-finite values.
Results may differ from a plain program's by a relative error of at most 0.013.
Values may be sent and summed in bfloat16 or wider, within the bound.
A program may use at most 128 MiB of HBM per device.

v0:
```python
import jax
import jax.numpy as jnp
from jax import lax
from jax.sharding import PartitionSpec as P

gelu_coef = 0.7978845608028654
cubic_coef = 0.044715


def tanh_gelu(pre_act):
    inner_arg = gelu_coef * (pre_act + cubic_coef * pre_act * pre_act * pre_act)
    return 0.5 * pre_act * (1.0 + jnp.tanh(inner_arg))


def tanh_gelu_slope(pre_act):
    inner_arg = gelu_coef * (pre_act + cubic_coef * pre_act * pre_act * pre_act)
    tanh_part = jnp.tanh(inner_arg)
    return 0.5 * (1.0 + tanh_part) + 0.5 * pre_act * (1.0 - tanh_part * tanh_part) * gelu_coef * (
        1.0 + 3.0 * cubic_coef * pre_act * pre_act
    )


def route_ranks(flat_routes):
    positions = jnp.arange(flat_routes.shape[0], dtype=jnp.int32)
    matches = (flat_routes[None, :] == flat_routes[:, None]) & (
        positions[None, :] < positions[:, None]
    )
    return jnp.sum(matches.astype(jnp.int32), axis=1)


def slot_table(flat_routes, experts_all, capacity):
    route_total = flat_routes.shape[0]
    ranking = route_ranks(flat_routes)
    kept_mask = ranking < capacity
    slot_index = jnp.where(kept_mask, flat_routes * capacity + ranking, experts_all * capacity)
    slot_route = jnp.full((experts_all * capacity + 1,), -1, jnp.int32)
    slot_route = slot_route.at[slot_index].set(jnp.arange(route_total, dtype=jnp.int32))
    return (slot_route[:-1], kept_mask, slot_index)


def per_device(tokens, routes, gates, cotangent, w_up, w_down):
    n_expert = lax.axis_size("expert")
    local_experts = w_up.shape[0]
    experts_all = local_experts * n_expert
    tok_rows = tokens.shape[0]
    top_k = routes.shape[1]
    model_width = tokens.shape[1]
    capacity = tok_rows * top_k // experts_all
    per_group = local_experts * capacity
    flat_routes = routes.reshape(-1)
    flat_gates = gates.reshape(-1)
    slot_route, kept_mask, slot_index = slot_table(flat_routes, experts_all, capacity)
    slot_valid = slot_route >= 0
    safe_route = jnp.where(slot_valid, slot_route, 0)
    token_ids = safe_route // top_k
    gate_vals = jnp.where(slot_valid, flat_gates[safe_route], jnp.float32(0.0))
    send_rows = jnp.where(slot_valid[:, None], tokens[token_ids], jnp.zeros((), jnp.bfloat16))
    send_rows = send_rows.reshape(n_expert, per_group, model_width)
    send_grads = (gate_vals[:, None] * cotangent[token_ids].astype(jnp.float32)).astype(
        jnp.bfloat16
    )
    send_grads = send_grads.reshape(n_expert, per_group, model_width)
    recv_rows = lax.all_to_all(send_rows, "expert", split_axis=0, concat_axis=0, tiled=True)
    grouped = recv_rows.reshape(n_expert, local_experts, capacity, model_width)
    pre_act = jnp.einsum("secd,edf->secf", grouped, w_up, preferred_element_type=jnp.float32)
    hidden = tanh_gelu(pre_act).astype(jnp.bfloat16)
    expert_out = jnp.einsum(
        "secf,efd->secd", hidden, w_down, preferred_element_type=jnp.float32
    ).astype(jnp.bfloat16)
    expert_out = expert_out.reshape(n_expert, per_group, model_width)
    back_out = lax.all_to_all(expert_out, "expert", split_axis=0, concat_axis=0, tiled=True)
    recv_grads = lax.all_to_all(send_grads, "expert", split_axis=0, concat_axis=0, tiled=True)
    grad_grouped = recv_grads.reshape(n_expert, local_experts, capacity, model_width)
    grad_hidden = jnp.einsum(
        "secd,efd->secf", grad_grouped, w_down, preferred_element_type=jnp.float32
    )
    grad_pre = (grad_hidden * tanh_gelu_slope(pre_act)).astype(jnp.bfloat16)
    grad_back = jnp.einsum(
        "secf,edf->secd", grad_pre, w_up, preferred_element_type=jnp.float32
    ).astype(jnp.bfloat16)
    grad_back = grad_back.reshape(n_expert, per_group, model_width)
    part_down = jnp.einsum(
        "secf,secd->efd", hidden, grad_grouped, preferred_element_type=jnp.float32
    )
    part_up = jnp.einsum("secd,secf->edf", grouped, grad_pre, preferred_element_type=jnp.float32)
    up_sum, down_sum = (
        lax.psum_scatter(
            part_up.astype(jnp.bfloat16), "dp", scatter_dimension=1, tiled=True
        ).astype(jnp.float32),
        lax.psum_scatter(
            part_down.astype(jnp.bfloat16), "dp", scatter_dimension=2, tiled=True
        ).astype(jnp.float32),
    )
    back_grad = lax.all_to_all(grad_back, "expert", split_axis=0, concat_axis=0, tiled=True)
    safe_slot = jnp.where(kept_mask, slot_index, 0)
    route_weight = jnp.where(kept_mask, flat_gates, jnp.float32(0.0))
    out_slots = back_out.reshape(experts_all * capacity, model_width)
    routed_out = out_slots[safe_slot].astype(jnp.float32) * route_weight[:, None]
    mixed = (
        tokens.astype(jnp.float32)
        + jnp.sum(routed_out.reshape(tok_rows, top_k, model_width), axis=1)
    ).astype(jnp.bfloat16)
    grad_slots = back_grad.reshape(experts_all * capacity, model_width)
    routed_grad = jnp.where(
        kept_mask[:, None], grad_slots[safe_slot].astype(jnp.float32), jnp.float32(0.0)
    )
    token_grad = (
        cotangent.astype(jnp.float32)
        + jnp.sum(routed_grad.reshape(tok_rows, top_k, model_width), axis=1)
    ).astype(jnp.bfloat16)
    return (mixed, token_grad, up_sum.astype(jnp.bfloat16), down_sum.astype(jnp.bfloat16))


def solution(mesh):
    return jax.shard_map(
        per_device,
        mesh=mesh,
        in_specs=(
            P(("expert", "dp"), None),
            P(("expert", "dp"), None),
            P(("expert", "dp"), None),
            P(("expert", "dp"), None),
            P("expert", None, None),
            P("expert", None, None),
        ),
        out_specs=(
            P(("expert", "dp"), None),
            P(("expert", "dp"), None),
            P("expert", "dp", None),
            P("expert", None, "dp"),
        ),
        check_vma=False,
    )
```

profile of v0, /device:TPU:0, one launch (start us, length us, event | category | flops | bytes accessed | tf_op | source)
XLA Modules:
  0.0 469.5 jit_solution(3350498697412716621)
XLA Ops:
  7.2 0.0 copy-start
  7.2 0.7 broadcast_multiply_fusion
  7.9 0.8 copy.22
  8.7 0.1 copy.23
  8.8 0.1 mul.86
  8.9 0.8 copy.26
  9.7 0.1 reshape.142
  9.8 0.1 eq.15
  9.9 0.5 convert_reduce_fusion
  10.4 4.3 scatter_custom_fusion
  14.8 4.5 gather_fusion.2
  19.3 0.0 copy-done
  19.3 6.1 %gather_fusion = bf16[1024,2048]{1,0:T(8,128)(2,1)} fusion(bf16[128,2048]{1,0:T(8,128)(2,1)S(1)} %copy-done, s32[1024]{0:T(1024)S(1)} %get-tuple-element.9), kind=kCustom, calls=%fused_computation | custom fusion | bytes 8392704 | tf_op jit(solution)/shard_map/gather | solution.py:57
  25.4 4.5 broadcast_select_fusion
  29.9 0.0 copy-start.1
  29.9 7.4 %all-to-all-start = ((bf16[8,128,2048]{2,1,0:T(8,128)(2,1)}), bf16[8,128,2048]{2,1,0:T(8,128)(2,1)}, u32[]{:S(2)}, u32[]{:S(2)}) async-start(bf16[8,128,2048]{2,1,0:T(8,128)(2,1)} %broadcast_select_fusion), calls=%async_computation | async-start | bytes 8388608 | tf_op jit(solution)/shard_map/all_to_all | solution.py:63
  37.3 0.0 copy-done.1
  37.3 6.1 %gather_fusion.3 = bf16[1024,2048]{1,0:T(8,128)(2,1)} fusion(bf16[128,2048]{1,0:T(8,128)(2,1)S(1)} %copy-done.1, s32[1024]{0:T(1024)S(1)} %get-tuple-element.9), kind=kCustom, calls=%fused_computation.3 | custom fusion | bytes 8392704 | tf_op jit(solution)/shard_map/gather | solution.py:59
  43.4 4.9 %fusion.1 = bf16[8,128,2048]{2,1,0:T(8,128)(2,1)} fusion(bf16[8,128,2048]{2,1,0:T(8,128)(2,1)} %bitcast.70, f32[8,128]{1,0:T(8,128)S(1)} %get-tuple-element.4), kind=kLoop, calls=%fused_computation.9 | loop fusion | flops 6291456 | bytes 8392704 | tf_op jit(solution)/shard_map/convert_element_type | solution.py:59
  48.2 82.3 %all-to-all-done = bf16[8,128,2048]{2,1,0:T(8,128)(2,1)} async-done(((bf16[8,128,2048]{2,1,0:T(8,128)(2,1)}), bf16[8,128,2048]{2,1,0:T(8,128)(2,1)}, u32[]{:S(2)}, u32[]{:S(2)}) %all-to-all-start) | async-done | bytes 4194336 | tf_op jit(solution)/shard_map/all_to_all | solution.py:63
  130.6 4.6 all-to-all-start.2
  135.2 0.0 reduce-scatter.3.cloned.1.call-start
  135.2 4.7 %fusion.24 = f32[8,8,16,128]{3,2,0,1:T(8,128)S(1)} fusion(bf16[8,2048,128]{2,1,0:T(8,128)(2,1)} %param.10, bf16[8,8,16,2048]{3,2,1,0:T(8,128)(2,1)} %bitcast.4), kind=kOutput, calls=%fused_computation.32 | convolution fusion | flops 536870912 | bytes 8912896 | tf_op jit(solution)/shard_map/secd,edf->secf/dot_general | solution.py:65
  139.9 87.8 %all-to-all-done.2 = bf16[8,128,2048]{2,1,0:T(8,128)(2,1)} async-done(((bf16[8,128,2048]{2,1,0:T(8,128)(2,1)}), bf16[8,128,2048]{2,1,0:T(8,128)(2,1)}, u32[]{:S(2)}, u32[]{:S(2)}) %all-to-all-start.2) | async-done | bytes 4194336 | tf_op jit(solution)/shard_map/all_to_all | solution.py:72
  227.7 4.9 %fusion.34 = bf16[8,8,16,128]{3,2,0,1:T(8,128)(2,1)S(1)} fusion(bf16[8,128,2048]{2,1,0:T(8,128)(2,1)} %param.11, bf16[8,8,16,2048]{3,2,1,0:T(8,128)(2,1)} %bitcast.17, f32[8,8,16,128]{3,2,0,1:T(8,128)S(1)} %fusion.24), kind=kOutput, calls=%fused_computation.34 | convolution fusion | flops 539361280 | bytes 9175040 | tf_op jit(solution)/shard_map/secd,efd->secf/dot_general | solution.py:74
  232.6 5.5 %bitcast_convert_fusion.1 = bf16[8,2048,128]{2,1,0:T(8,128)(2,1)} fusion(bf16[8,8,16,2048]{3,2,1,0:T(8,128)(2,1)} %bitcast.4, bf16[8,8,16,128]{3,2,0,1:T(8,128)(2,1)S(1)} %fusion.34), kind=kOutput, calls=%fused_computation.13 | convolution fusion | flops 538968064 | bytes 8650752 | tf_op jit(solution)/shard_map/secd,secf->edf/dot_general | solution.py:85
  238.2 0.0 reduce-scatter.3.cloned.1.call-update
  238.2 3.4 convert_bitcast_fusion.1
  241.7 2.3 copy.25
  244.0 4.9 %all-to-all-start.1 = ((bf16[8,128,2048]{2,1,0:T(8,128)(2,1)}), bf16[8,128,2048]{2,1,0:T(8,128)(2,1)}, u32[]{:S(2)}, u32[]{:S(2)}) async-start(bf16[8,128,2048]{2,1,0:T(8,128)(2,1)} %bitcast.72), calls=%async_computation.1 | async-start | bytes 8388608 | tf_op jit(solution)/shard_map/all_to_all | solution.py:71
  248.8 3.4 convert_bitcast_fusion
  252.3 2.5 copy.29
  254.8 86.3 %all-to-all-done.1 = bf16[8,128,2048]{2,1,0:T(8,128)(2,1)} async-done(((bf16[8,128,2048]{2,1,0:T(8,128)(2,1)}), bf16[8,128,2048]{2,1,0:T(8,128)(2,1)}, u32[]{:S(2)}, u32[]{:S(2)}) %all-to-all-start.1) | async-done | bytes 4194336 | tf_op jit(solution)/shard_map/all_to_all | solution.py:71
  341.1 4.5 all-to-all-start.3
  345.6 0.0 reduce-scatter.5.cloned.1.call-start
  345.7 5.4 %bitcast_convert_fusion = bf16[8,128,2048]{2,1,0:T(8,128)(2,1)} fusion(bf16[8,8,16,2048]{3,2,1,0:T(8,128)(2,1)} %bitcast.17, f32[8,8,16,128]{3,2,0,1:T(8,128)S(1)} %fusion.24), kind=kOutput, calls=%fused_computation.12 | convolution fusion | flops 540147712 | bytes 8912896 | tf_op jit(solution)/shard_map/secf,secd->efd/dot_general | solution.py:82
  351.1 0.0 reduce-scatter.5.cloned.1.call-update
  351.2 0.1 lt.72
  351.3 11.6 %gather_fusion.1 = bf16[1024,2048]{1,0:T(8,128)(2,1)} fusion(bf16[1024,2048]{1,0:T(8,128)(2,1)} %bitcast.12, s32[1024]{0:T(1024)S(1)} %broadcast_clamp_fusion), kind=kCustom, calls=%fused_computation.1 | custom fusion | bytes 8392704 | tf_op jit(solution)/shard_map/gather | solution.py:98
  362.9 75.2 %all-to-all-done.3 = bf16[8,128,2048]{2,1,0:T(8,128)(2,1)} async-done(((bf16[8,128,2048]{2,1,0:T(8,128)(2,1)}), bf16[8,128,2048]{2,1,0:T(8,128)(2,1)}, u32[]{:S(2)}, u32[]{:S(2)}) %all-to-all-start.3) | async-done | bytes 4194336 | tf_op jit(solution)/shard_map/all_to_all | solution.py:94
  438.1 11.6 %gather_fusion.4 = bf16[1024,2048]{1,0:T(8,128)(2,1)} fusion(bf16[1024,2048]{1,0:T(8,128)(2,1)} %bitcast.23, s32[1024]{0:T(1024)S(1)} %broadcast_clamp_fusion), kind=kCustom, calls=%fused_computation.4 | custom fusion | bytes 8392704 | tf_op jit(solution)/shard_map/gather | solution.py:105
  449.6 0.0 copy-start.2
  449.6 6.7 %fusion.2 = f32[128,2048]{1,0:T(8,128)S(1)} fusion(bf16[1024,2048]{1,0:T(8,128)(2,1)} %gather_fusion.1, f32[128,8]{1,0:T(8,128)S(1)} %broadcast_select_fusion.1), kind=kLoop, calls=%fused_computation.11 | loop fusion | flops 6029312 | bytes 5246976 | tf_op jit(solution)/shard_map/reduce_sum | solution.py:101
  456.3 0.0 copy-done.2
  456.3 4.5 fusion
  460.8 0.9 add_convert_fusion.1
  461.7 0.9 add_convert_fusion
  462.6 0.0 reduce-scatter.3.cloned.1.call-done
  (8 shorter events, 0.1 us)
Async XLA Ops:
  7.2 12.2 %copy-start = (bf16[128,2048]{1,0:T(8,128)(2,1)S(1)}, bf16[128,2048]{1,0:T(8,128)(2,1)}, u32[]{:S(2)}) copy-start(bf16[128,2048]{1,0:T(8,128)(2,1)} %param.6) | copy-start | bytes 1572868
  29.9 7.4 %copy-start.1 = (bf16[128,2048]{1,0:T(8,128)(2,1)S(1)}, bf16[128,2048]{1,0:T(8,128)(2,1)}, u32[]{:S(2)}) copy-start(bf16[128,2048]{1,0:T(8,128)(2,1)} %param.9) | copy-start | bytes 1572868
  29.9 100.7 %all-to-all-start = ((bf16[8,128,2048]{2,1,0:T(8,128)(2,1)}), bf16[8,128,2048]{2,1,0:T(8,128)(2,1)}, u32[]{:S(2)}, u32[]{:S(2)}) async-start(bf16[8,128,2048]{2,1,0:T(8,128)(2,1)} %broadcast_select_fusion), calls=%async_computation | async-start | bytes 8388608 | tf_op jit(solution)/shard_map/all_to_all | solution.py:63
  130.6 97.1 %all-to-all-start.2 = ((bf16[8,128,2048]{2,1,0:T(8,128)(2,1)}), bf16[8,128,2048]{2,1,0:T(8,128)(2,1)}, u32[]{:S(2)}, u32[]{:S(2)}) async-start(bf16[8,128,2048]{2,1,0:T(8,128)(2,1)} %fusion.1), calls=%async_computation.2 | async-start | bytes 8388608 | tf_op jit(solution)/shard_map/all_to_all | solution.py:72
  135.2 327.5 %reduce-scatter.3.cloned.1.call-start = ((), (), s32[]{:S(2)}) async-start(), calls=%async_computation.6 | async-start | bytes 5242880 | tf_op jit(solution)/shard_map/reduce_scatter | solution.py:87
  244.0 97.1 %all-to-all-start.1 = ((bf16[8,128,2048]{2,1,0:T(8,128)(2,1)}), bf16[8,128,2048]{2,1,0:T(8,128)(2,1)}, u32[]{:S(2)}, u32[]{:S(2)}) async-start(bf16[8,128,2048]{2,1,0:T(8,128)(2,1)} %bitcast.72), calls=%async_computation.1 | async-start | bytes 8388608 | tf_op jit(solution)/shard_map/all_to_all | solution.py:71
  341.1 97.0 %all-to-all-start.3 = ((bf16[8,128,2048]{2,1,0:T(8,128)(2,1)}), bf16[8,128,2048]{2,1,0:T(8,128)(2,1)}, u32[]{:S(2)}, u32[]{:S(2)}) async-start(bf16[8,128,2048]{2,1,0:T(8,128)(2,1)} %bitcast.71), calls=%async_computation.3 | async-start | bytes 8388608 | tf_op jit(solution)/shard_map/all_to_all | solution.py:94
  345.6 117.0 %reduce-scatter.5.cloned.1.call-start = ((), (), s32[]{:S(2)}) async-start(), calls=%async_computation.7 | async-start | bytes 5242880 | tf_op jit(solution)/shard_map/reduce_scatter | solution.py:90
  449.6 6.7 %copy-start.2 = (bf16[1024,2048]{1,0:T(8,128)(2,1)S(1)}, bf16[1024,2048]{1,0:T(8,128)(2,1)}, u32[]{:S(2)}) copy-start(bf16[1024,2048]{1,0:T(8,128)(2,1)} %gather_fusion.4) | copy-start | bytes 12582916
Sparse Core Ops, SparseCore 0:
  238.3 43.6 reduce-scatter.2
  351.3 45.6 reduce-scatter.4
where the time goes:
time: 470 us; the launch traced here: 469 us
  waiting for transfers between devices  332 us (71%)
  local copies, waits for them, and re-layouts  50.9 us (11%)
  matrix products  27.5 us (6%)
  other arithmetic  23.7 us (5%)
  starting transfers between devices  21.5 us (5%)
  between operations  14.2 us (3%)
    all_to_all x1, waiting for transfers between devices, per_device(): lax.all_to_all(send_grads, 'expert', split_axis=0, concat_axis=0, tiled=T...  87.8 us
    all_to_all x1, waiting for transfers between devices, per_device(): lax.all_to_all(expert_out, 'expert', split_axis=0, concat_axis=0, tiled=T...  86.3 us
    all_to_all x1, waiting for transfers between devices, per_device(): lax.all_to_all(send_rows, 'expert', split_axis=0, concat_axis=0, tiled=True)  82.3 us
    all_to_all x1, waiting for transfers between devices, per_device(): lax.all_to_all(grad_back, 'expert', split_axis=0, concat_axis=0, tiled=True)  75.2 us
    gather x1, local copies, waits for them, and re-layouts, per_device(): out_slots[safe_slot].astype(jnp.float32) * route_weight[:, None]  11.6 us
    gather x1, local copies, waits for them, and re-layouts, per_device(): grad_slots[safe_slot].astype(jnp.float32)  11.6 us
  transfers between devices with their start and end apart: 6, of which 4 were waited for; matrix products, arithmetic and copies ran while one was open for 15% of the time, Pallas kernels for 0%

commit v1 on v0

v1 whole, which is shorter than its diff:
```python
import jax
import jax.numpy as jnp
from jax import lax
from jax.sharding import PartitionSpec as P

gelu_coef = 0.7978845608028654
cubic_coef = 0.044715


def gelu_and_slope(pre_act):
    square = pre_act * pre_act
    tanh_part = jnp.tanh(gelu_coef * pre_act * (1.0 + cubic_coef * square))
    value = 0.5 * pre_act * (1.0 + tanh_part)
    slope = 0.5 * (1.0 + tanh_part) + 0.5 * pre_act * (1.0 - tanh_part * tanh_part) * gelu_coef * (
        1.0 + 3.0 * cubic_coef * square
    )
    return value, slope


def kept_gates(routes, gates, experts_all, capacity):
    tok_rows = routes.shape[0]
    hits = routes[:, :, None] == jnp.arange(experts_all, dtype=jnp.int32)[None, None, :]
    named = jnp.any(hits, axis=1)
    gate_of = jnp.sum(jnp.where(hits, gates[:, :, None], jnp.float32(0.0)), axis=1)
    earlier = jnp.tril(jnp.ones((tok_rows, tok_rows), jnp.bfloat16), -1)
    rank = jnp.dot(earlier, named.astype(jnp.bfloat16), preferred_element_type=jnp.float32)
    return jnp.where(named & (rank < capacity), gate_of, jnp.float32(0.0))


def per_device(tokens, routes, gates, cotangent, w_up, w_down):
    n_expert = lax.axis_size("expert")
    local_experts, model_width, hidden_width = w_up.shape
    experts_all = local_experts * n_expert
    tok_rows = tokens.shape[0]
    top_k = routes.shape[1]
    capacity = tok_rows * top_k // experts_all
    rows_all = n_expert * tok_rows
    units = local_experts * hidden_width

    gate_full = kept_gates(routes, gates, experts_all, capacity)
    gate_hi = gate_full.astype(jnp.bfloat16)
    gate_lo = (gate_full - gate_hi.astype(jnp.float32)).astype(jnp.bfloat16)
    gate_pair = jnp.concatenate([gate_hi, gate_lo], axis=1)

    all_tokens = lax.all_gather(tokens, "expert", axis=0, tiled=True)
    all_cot = lax.all_gather(
        jnp.concatenate([cotangent, gate_pair], axis=1), "expert", axis=0, tiled=True
    )
    first = lax.axis_index("expert") * local_experts
    all_gates = lax.dynamic_slice_in_dim(
        all_cot, model_width + first, local_experts, axis=1
    ).astype(jnp.float32) + lax.dynamic_slice_in_dim(
        all_cot, model_width + experts_all + first, local_experts, axis=1
    ).astype(jnp.float32)
    all_cot = all_cot[:, :model_width]
    gate_units = all_gates[:, :, None]

    pre_act = jnp.einsum("td,edf->tef", all_tokens, w_up, preferred_element_type=jnp.float32)
    value, slope = gelu_and_slope(pre_act)
    weighted = (value * gate_units).astype(jnp.bfloat16)
    mixed_part = jnp.einsum(
        "tef,efd->td", weighted, w_down, preferred_element_type=jnp.float32
    ).astype(jnp.bfloat16)
    mixed_sum = lax.psum_scatter(mixed_part, "expert", scatter_dimension=0, tiled=True)

    grad_hidden = jnp.einsum("td,efd->tef", all_cot, w_down, preferred_element_type=jnp.float32)
    grad_pre = (grad_hidden * slope * gate_units).astype(jnp.bfloat16)
    grad_part = jnp.einsum(
        "tef,edf->td", grad_pre, w_up, preferred_element_type=jnp.float32
    ).astype(jnp.bfloat16)
    grad_sum = lax.psum_scatter(grad_part, "expert", scatter_dimension=0, tiled=True)

    part_up = jnp.einsum(
        "td,tef->edf", all_tokens, grad_pre, preferred_element_type=jnp.float32
    ).astype(jnp.bfloat16)
    part_down = jnp.einsum(
        "tef,td->efd", weighted, all_cot, preferred_element_type=jnp.float32
    ).astype(jnp.bfloat16)
    up_sum = lax.psum_scatter(part_up, "dp", scatter_dimension=1, tiled=True)
    down_sum = lax.psum_scatter(part_down, "dp", scatter_dimension=2, tiled=True)

    mixed = (tokens.astype(jnp.float32) + mixed_sum.astype(jnp.float32)).astype(jnp.bfloat16)
    token_grad = (cotangent.astype(jnp.float32) + grad_sum.astype(jnp.float32)).astype(
        jnp.bfloat16
    )
    return (mixed, token_grad, up_sum, down_sum)


def solution(mesh):
    return jax.shard_map(
        per_device,
        mesh=mesh,
        in_specs=(
            P(("expert", "dp"), None),
            P(("expert", "dp"), None),
            P(("expert", "dp"), None),
            P(("expert", "dp"), None),
            P("expert", None, None),
            P("expert", None, None),
        ),
        out_specs=(
            P(("expert", "dp"), None),
            P(("expert", "dp"), None),
            P("expert", "dp", None),
            P("expert", None, "dp"),
        ),
        check_vma=False,
    )
```

time: 470 us -> 462 us (0.983)
  waiting for transfers between devices: 332 us -> 382 us
  local copies, waits for them, and re-layouts: 50.9 us -> 3.58 us
  matrix products: 27.5 us -> 54.6 us
  starting transfers between devices: 21.5 us -> 0.42 us
  other arithmetic: 23.7 us -> 6.98 us
    all_to_all x4 -> x0, waiting for transfers between devices: 332 us -> none  [the longest x1 87.8 us: per_device(): lax.all_to_all(send_grads, 'expert', split_axis=0, concat_axis=0, tiled=T...]
    reduce_scatter x2 -> x4, waiting for transfers between devices: 0.01 us -> 238 us  [the longest x1 89.6 us: per_device(): lax.psum_scatter(mixed_part, 'expert', scatter_dimension=0, tiled=True)]
    all_gather x0 -> x2, waiting for transfers between devices: none -> 143 us  [the longest x1 73.7 us: per_device(): all_tokens = lax.all_gather(tokens, 'expert', axis=0, tiled=True)]
    gather x5 -> x0, local copies, waits for them, and re-layouts: 39.8 us -> none  [the longest x1 11.6 us: per_device(): out_slots[safe_slot].astype(jnp.float32) * route_weight[:, None]]
    dot_general x6 -> x7, matrix products: 27.5 us -> 54.6 us  [the longest x1 10.5 us: per_device(): jnp.einsum('tef,td->efd', weighted, all_cot, preferred_element_type=jnp.f...]
    all_to_all x4 -> x0, starting transfers between devices: 21.4 us -> none  [the longest x1 7.41 us: per_device(): lax.all_to_all(send_rows, 'expert', split_axis=0, concat_axis=0, tiled=True)]
    reduce_sum x3 -> x1, other arithmetic: 11.7 us -> 0.74 us  [kept_gates(): jnp.sum(jnp.where(hits, gates[:, :, None], jnp.float32(0.0)), axis=1)]
    convert_element_type x2 -> x0, local copies, waits for them, and re-layouts: 4.78 us -> none  [the longest x1 2.47 us: per_device(): grad_back = jnp.einsum('secf,edf->secd', grad_pre, w_up, preferred_elemen...]
  transfers between devices with their start and end apart: 6 -> 6, of which waited for: 4 -> 6; matrix products, arithmetic and copies ran while one was open for 15% -> 10% of each run, Pallas kernels for 0% -> 0%
where the time goes in v1:
time: 462 us
  waiting for transfers between devices  382 us (83%)
  matrix products  54.6 us (12%)
  between operations  14.2 us (3%)
  other arithmetic  6.98 us (2%)
    reduce_scatter x1, waiting for transfers between devices, per_device(): lax.psum_scatter(mixed_part, 'expert', scatter_dimension=0, tiled=True)  89.6 us
    reduce_scatter x1, waiting for transfers between devices, per_device(): lax.psum_scatter(grad_part, 'expert', scatter_dimension=0, tiled=True)  89.5 us
    all_gather x1, waiting for transfers between devices, per_device(): all_tokens = lax.all_gather(tokens, 'expert', axis=0, tiled=True)  73.7 us
    all_gather x1, waiting for transfers between devices, per_device(): lax.all_gather(jnp.concatenate([cotangent, gate_pair], axis=1), 'expert',...  68.9 us
    reduce_scatter x1, waiting for transfers between devices, per_device(): lax.psum_scatter(part_down, 'dp', scatter_dimension=2, tiled=True)  45.1 us
    reduce_scatter x1, waiting for transfers between devices, per_device(): up_sum = lax.psum_scatter(part_up, 'dp', scatter_dimension=1, tiled=True)  14.3 us
    dot_general x1, matrix products, per_device(): jnp.einsum('tef,td->efd', weighted, all_cot, preferred_element_type=jnp.f...  10.5 us
    dot_general x1, matrix products, per_device(): jnp.einsum('td,efd->tef', all_cot, w_down, preferred_element_type=jnp.flo...  10.3 us
  transfers between devices with their start and end apart: 6, of which 6 were waited for; matrix products, arithmetic and copies ran while one was open for 10% of the time, Pallas kernels for 0%

profile of v1, /device:TPU:0, one launch (start us, length us, event | category | flops | bytes accessed | tf_op | source)
XLA Modules:
  0.0 461.5 jit_solution(14571028824377396124)
XLA Ops:
  7.2 0.0 all-gather.3.cloned.1.call-start
  7.2 0.7 all-gather.3.cloned.1.call-update
  7.9 0.0 all-gather.5.cloned.1.call-start
  7.9 1.3 copy.24
  9.3 0.7 fusion.9
  10.0 0.7 select_reduce_fusion
  10.7 0.2 subtract_convert_fusion
  11.0 0.8 pad_maximum_fusion
  11.8 0.0 all-gather.5.cloned.1.call-update
  11.8 0.0 reduce-scatter.9.cloned.1.call-start
  11.9 73.7 %all-gather.3.cloned.1.call-done = bf16[1024,2048]{1,0:T(8,128)(2,1)} async-done(((bf16[128,2048]{1,0:T(8,128)(2,1)}), bf16[1024,2048]{1,0:T(8,128)(2,1)}) %all-gather.3.cloned.1.call-update) | async-done | bytes 4194320 | tf_op jit(solution)/shard_map/all_gather | solution.py:45
  85.6 9.9 %fusion.2 = f32[1024,8,128]{2,0,1:T(8,128)} fusion(bf16[8,2048,128]{2,1,0:T(8,128)(2,1)} %param.10, bf16[1024,2048]{1,0:T(8,128)(2,1)} %all-gather.3.cloned.1.call-done), kind=kOutput, calls=%fused_computation.5 | convolution fusion | flops 4294967296 | bytes 12582912 | tf_op jit(solution)/shard_map/td,edf->tef/dot_general | solution.py:58
  95.6 68.9 %all-gather.5.cloned.1.call-done = bf16[1024,2176]{0,1:T(8,128)(2,1)} async-done(((bf16[128,2176]{0,1:T(8,128)(2,1)}), bf16[1024,2176]{0,1:T(8,128)(2,1)}) %all-gather.5.cloned.1.call-update) | async-done | bytes 4456464 | tf_op jit(solution)/shard_map/all_gather | solution.py:46
  164.4 0.7 convert_add_fusion
  165.2 0.0 copy-start.2
  165.2 10.3 %multiply_convert_fusion = bf16[1024,8,128]{2,0,1:T(8,128)(2,1)S(1)} fusion(f32[1024,8,128]{2,0,1:T(8,128)} %fusion.2, bf16[8,128,2048]{2,1,0:T(8,128)(2,1)} %param.11, bf16[1024,2176]{0,1:T(8,128)(2,1)} %all-gather.5.cloned.1.call-done, f32[1024,8]{0,1:T(8,128)S(1)} %convert_add_fusion), kind=kOutput, calls=%fused_computation.8 | convolution fusion | flops 4314890240 | bytes 14712832 | tf_op jit(solution)/shard_map/td,efd->tef/dot_general | solution.py:66
  175.5 0.0 copy-done.2
  175.5 6.1 %convert_bitcast_fusion = bf16[8,2048,128]{1,2,0:T(8,128)(2,1)} fusion(bf16[1024,8,128]{2,0,1:T(8,128)(2,1)S(1)} %multiply_convert_fusion, bf16[1024,2048]{1,0:T(8,128)(2,1)S(1)} %copy-done.2), kind=kOutput, calls=%fused_computation.7 | convolution fusion | flops 4297064448 | bytes 10485760 | tf_op jit(solution)/shard_map/td,tef->edf/dot_general | solution.py:73
  181.6 0.0 reduce-scatter.9.cloned.1.call-update
  181.6 0.0 reduce-scatter.5.cloned.1.call-start
  181.7 9.3 %bitcast_convert_fusion.1 = bf16[1024,2048]{1,0:T(8,128)(2,1)} fusion(bf16[8,128,2048]{2,1,0:T(8,128)(2,1)} %param.11, f32[1024,8,128]{2,0,1:T(8,128)} %fusion.2, f32[1024,8]{0,1:T(8,128)S(1)} %convert_add_fusion), kind=kOutput, calls=%fused_computation.1 | convolution fusion | flops 4307550208 | bytes 12615680 | tf_op jit(solution)/shard_map/tef,efd->td/dot_general | solution.py:61
  191.0 0.0 reduce-scatter.5.cloned.1.call-update
  191.0 0.2 reduce-scatter.7.cloned.1.call-start
  191.3 8.3 %bitcast_convert_fusion = bf16[1024,2048]{1,0:T(8,128)(2,1)} fusion(bf16[1024,8,128]{2,0,1:T(8,128)(2,1)S(1)} %multiply_convert_fusion, bf16[8,2048,128]{2,1,0:T(8,128)(2,1)} %param.10), kind=kOutput, calls=%fused_computation | convolution fusion | flops 4297064448 | bytes 10485760 | tf_op jit(solution)/shard_map/tef,edf->td/dot_general | solution.py:68
  199.5 0.0 reduce-scatter.7.cloned.1.call-update
  199.6 0.0 reduce-scatter.11.cloned.1.call-start
  199.6 10.5 %convolution_convert_fusion = bf16[8,128,2048]{2,1,0:T(8,128)(2,1)} fusion(bf16[1024,2176]{0,1:T(8,128)(2,1)} %all-gather.5.cloned.1.call-done, f32[1024,8,128]{2,0,1:T(8,128)} %fusion.2, f32[1024,8]{0,1:T(8,128)S(1)} %convert_add_fusion), kind=kOutput, calls=%fused_computation.11 | convolution fusion | flops 4307550208 | bytes 12615680 | tf_op jit(solution)/shard_map/tef,td->efd/dot_general | solution.py:76
  210.1 0.0 copy-start
  210.1 0.0 copy-start.1
  210.1 0.0 reduce-scatter.11.cloned.1.call-update
  210.1 14.3 %reduce-scatter.9.cloned.1.call-done = bf16[8,512,128]{1,2,0:T(8,128)(2,1)} async-done(((bf16[8,2048,128]{1,2,0:T(8,128)(2,1)}), bf16[8,512,128]{1,2,0:T(8,128)(2,1)}) %reduce-scatter.9.cloned.1.call-update) | async-done | bytes 1048592 | tf_op jit(solution)/shard_map/reduce_scatter | solution.py:79
  224.4 2.3 copy.29
  226.7 89.6 %reduce-scatter.5.cloned.1.call-done = bf16[128,2048]{1,0:T(8,128)(2,1)} async-done(((bf16[1024,2048]{1,0:T(8,128)(2,1)}), bf16[128,2048]{1,0:T(8,128)(2,1)}) %reduce-scatter.5.cloned.1.call-update) | async-done | bytes 524304 | tf_op jit(solution)/shard_map/reduce_scatter | solution.py:64
  316.2 0.0 copy-done
  316.2 2.0 add_convert_fusion.1
  318.2 89.5 %reduce-scatter.7.cloned.1.call-done = bf16[128,2048]{1,0:T(8,128)(2,1)} async-done(((bf16[1024,2048]{1,0:T(8,128)(2,1)}), bf16[128,2048]{1,0:T(8,128)(2,1)}) %reduce-scatter.7.cloned.1.call-update) | async-done | bytes 524304 | tf_op jit(solution)/shard_map/reduce_scatter | solution.py:71
  407.6 0.0 copy-done.1
  407.6 2.0 add_convert_fusion
  409.6 45.1 %reduce-scatter.11.cloned.1.call-done = bf16[8,128,512]{2,1,0:T(8,128)(2,1)} async-done(((bf16[8,128,2048]{2,1,0:T(8,128)(2,1)}), bf16[8,128,512]{2,1,0:T(8,128)(2,1)}) %reduce-scatter.11.cloned.1.call-update) | async-done | bytes 1048592 | tf_op jit(solution)/shard_map/reduce_scatter | solution.py:80
  (1 shorter events, 0.0 us)
Async XLA Ops:
  7.2 78.5 %all-gather.3.cloned.1.call-start = ((), (), s32[]{:S(2)}) async-start(), calls=%async_computation.4 | async-start | bytes 4718592 | tf_op jit(solution)/shard_map/all_gather | solution.py:45
  7.9 156.5 %all-gather.5.cloned.1.call-start = ((), (), s32[]{:S(2)}) async-start(), calls=%async_computation.5 | async-start | bytes 5013504 | tf_op jit(solution)/shard_map/all_gather | solution.py:46
  11.8 212.5 %reduce-scatter.9.cloned.1.call-start = ((), (), s32[]{:S(2)}) async-start(), calls=%async_computation.8 | async-start | bytes 5242880 | tf_op jit(solution)/shard_map/reduce_scatter | solution.py:79
  165.2 10.3 %copy-start.2 = (bf16[1024,2048]{1,0:T(8,128)(2,1)S(1)}, bf16[1024,2048]{1,0:T(8,128)(2,1)}, u32[]{:S(2)}) copy-start(bf16[1024,2048]{1,0:T(8,128)(2,1)} %all-gather.3.cloned.1.call-done) | copy-start | bytes 12582916
  181.6 134.6 %reduce-scatter.5.cloned.1.call-start = ((), (), s32[]{:S(2)}) async-start(), calls=%async_computation.6 | async-start | bytes 4718592 | tf_op jit(solution)/shard_map/reduce_scatter | solution.py:64
  191.0 216.6 %reduce-scatter.7.cloned.1.call-start = ((), (), s32[]{:S(2)}) async-start(), calls=%async_computation.7 | async-start | bytes 4718592 | tf_op jit(solution)/shard_map/reduce_scatter | solution.py:71
  199.6 255.1 %reduce-scatter.11.cloned.1.call-start = ((), (), s32[]{:S(2)}) async-start(), calls=%async_computation.9 | async-start | bytes 5242880 | tf_op jit(solution)/shard_map/reduce_scatter | solution.py:80
  210.1 106.1 %copy-start = (bf16[128,2048]{1,0:T(8,128)(2,1)S(1)}, bf16[128,2048]{1,0:T(8,128)(2,1)}, u32[]{:S(2)}) copy-start(bf16[128,2048]{1,0:T(8,128)(2,1)} %param.6) | copy-start | bytes 1572868
  210.1 197.6 %copy-start.1 = (bf16[128,2048]{1,0:T(8,128)(2,1)S(1)}, bf16[128,2048]{1,0:T(8,128)(2,1)}, u32[]{:S(2)}) copy-start(bf16[128,2048]{1,0:T(8,128)(2,1)} %param.9) | copy-start | bytes 1572868
Sparse Core Ops, SparseCore 0:
  10.1 75.4 all-gather.2
  88.3 76.1 all-gather.4
  181.7 42.5 reduce-scatter.8
  227.9 88.2 reduce-scatter.4
  319.7 87.9 reduce-scatter.6
  410.6 44.0 reduce-scatter.10

commit v2 on v1

--- a/solution.py
+++ b/solution.py
@@ -2,6 +2,7 @@
 import jax.numpy as jnp
 from jax import lax
 from jax.sharding import PartitionSpec as P
+
 
 gelu_coef = 0.7978845608028654
 cubic_coef = 0.044715
@@ -27,15 +28,187 @@
     return jnp.where(named & (rank < capacity), gate_of, jnp.float32(0.0))
 
 
+def shifted(value, axis, table):
+    return lax.ppermute(value, axis, table)
+
+
+def after(value, *others):
+    return lax.optimization_barrier((value,) + others)[0]
+
+
+def shift_table(outer, inner, outer_by, inner_by):
+    pairs = []
+    for a in range(outer):
+        for b in range(inner):
+            to = (a + outer_by) % outer * inner + (b + inner_by) % inner
+            pairs.append((a * inner + b, to))
+    return pairs
+
+
 def per_device(tokens, routes, gates, cotangent, w_up, w_down):
-    n_expert = lax.axis_size("expert")
-    local_experts, model_width, hidden_width = w_up.shape
+    n_expert, n_dp = lax.axis_size("expert"), lax.axis_size("dp")
+    cores = 2
+    n_x = n_dp // cores
+    n_z = n_expert // n_x
+    local_experts, model_width, _ = w_up.shape
     experts_all = local_experts * n_expert
     tok_rows = tokens.shape[0]
     top_k = routes.shape[1]
     capacity = tok_rows * top_k // experts_all
-    rows_all = n_expert * tok_rows
-    units = local_experts * hidden_width
+    first = lax.axis_index("expert") * local_experts
+
+    def z_shift(block, by):
+        return shifted(block, "expert", shift_table(n_z, n_x, by, 0))
+
+    def x_shift(block, by):
+        return shifted(block, "expert", shift_table(n_z, n_x, 0, by))
+
+    z_order = sorted(range(1, n_z), key=lambda by: min(by, n_z - by))
+
+    def gather_both(rows, cots):
+        row_of, cot_of = {(0, 0): rows}, {(0, 0): cots}
+        for sx in range(1, n_x):
+            row_of[sx, 0] = x_shift(rows, sx)
+            cot_of[sx, 0] = x_shift(after(cots, row_of[sx, 0]), sx)
+        for by in z_order:
+            row_of[0, by] = z_shift(rows, by)
+        near, far = z_order[:-1], z_order[-1]
+        for by in near:
+            cot_of[0, by] = z_shift(after(cots, *[row_of[0, b] for b in near]), by)
+        last = cot_of[n_x - 1, 0]
+        for by in z_order:
+            for sx in range(1, n_x):
+                row_of[sx, by] = x_shift(after(row_of[0, by], last), sx)
+        cot_of[0, far] = z_shift(after(cots, row_of[0, far]), far)
+        for by in z_order:
+            for sx in range(1, n_x):
+                cot_of[sx, by] = x_shift(cot_of[0, by], sx)
+        for part in (row_of, cot_of):
+            part[0, far] = after(part[0, far], *[part[n_x - 1, by] for by in near])
+        return [
+            [
+                jnp.concatenate([part[sx, sz] for sz in range(n_z)], axis=0)
+                for sx in range(n_x)
+            ]
+            for part in (row_of, cot_of)
+        ]
+
+    def scatter(parts):
+        def total(sz, *earlier):
+            rows = slice(sz * tok_rows, (sz + 1) * tok_rows)
+            value = parts[0][rows].astype(jnp.float32)
+            for item in sent[sz]:
+                value = value + after(item, *earlier).astype(jnp.float32)
+            return value
+
+        sent = {}
+        for sz in z_order + [0]:
+            rows = slice(sz * tok_rows, (sz + 1) * tok_rows)
+            sent[sz] = [x_shift(parts[sx][rows], -sx) for sx in range(1, n_x)]
+        arrived = []
+        for sz in z_order:
+            column = total(sz, *arrived[-1:]).astype(jnp.bfloat16)
+            arrived.append(z_shift(column, -sz))
+        return total(0), arrived
+
+    def summed(own, arrived):
+        for item in arrived:
+            own = own + item.astype(jnp.float32)
+        return own
+
+    def reduce_dp(part, axis):
+        n_y = n_dp // cores
+        core = lax.axis_index("dp") % cores
+        level = lax.axis_index("dp") // cores
+        width = part.shape[axis] // n_dp
+
+        def piece(y, c):
+            return lax.dynamic_slice_in_dim(part, (y * cores + c) * width, width, axis)
+
+        sums = []
+        for sy in range(n_y):
+            y = (level + sy) % n_y
+            sent = shifted(piece(y, 1 - core), "dp", shift_table(n_y, cores, 0, 1))
+            sums.append(piece(y, core).astype(jnp.float32) + sent.astype(jnp.float32))
+        result = sums[0]
+        for sy in range(1, n_y):
+            sent = shifted(
+                sums[sy].astype(jnp.bfloat16), "dp", shift_table(n_y, cores, sy, 0)
+            )
+            result = result + sent.astype(jnp.float32)
+        return result.astype(jnp.bfloat16)
+
+    gate_full = kept_gates(routes, gates, experts_all, capacity)
+    gate_hi = gate_full.astype(jnp.bfloat16)
+    gate_lo = (gate_full - gate_hi.astype(jnp.float32)).astype(jnp.bfloat16)
+    with_gates, cots = gather_both(
+        jnp.concatenate([tokens, gate_hi, gate_lo], axis=1), cotangent
+    )
+
+    slopes, weights_of, rows_of, mixed_parts = [], [], [], []
+    for chunk in with_gates:
+        gate_units = (
+            lax.dynamic_slice_in_dim(chunk, model_width + first, local_experts, axis=1).astype(
+                jnp.float32
+            )
+            + lax.dynamic_slice_in_dim(
+                chunk, model_width + experts_all + first, local_experts, axis=1
+            ).astype(jnp.float32)
+        )[:, :, None]
+        rows = chunk[:, :model_width]
+        pre_act = jnp.einsum("td,edf->tef", rows, w_up, preferred_element_type=jnp.float32)
+        value, slope = gelu_and_slope(pre_act)
+        weighted = (value * gate_units).astype(jnp.bfloat16)
+        mixed_parts.append(
+            jnp.einsum("tef,efd->td", weighted, w_down, preferred_element_type=jnp.float32).astype(
+                jnp.bfloat16
+            )
+        )
+        slopes.append(slope * gate_units)
+        weights_of.append(weighted)
+        rows_of.append(rows)
+    mixed_own, mixed_arrived = scatter(mixed_parts)
+    mixed_sum = summed(mixed_own, mixed_arrived)
+
+    grad_pres, grad_parts = [], []
+    for slope, rows in zip(slopes, cots):
+        grad_hidden = jnp.einsum("td,efd->tef", rows, w_down, preferred_element_type=jnp.float32)
+        grad_pre = (grad_hidden * slope).astype(jnp.bfloat16)
+        grad_parts.append(
+            jnp.einsum("tef,edf->td", grad_pre, w_up, preferred_element_type=jnp.float32).astype(
+                jnp.bfloat16
+            )
+        )
+        grad_pres.append(grad_pre)
+    grad_own, grad_arrived = scatter(grad_parts)
+    grad_sum = summed(grad_own, grad_arrived)
+
+    weights_of = [after(item, mixed_arrived[0]) for item in weights_of]
+    rows_of = [after(item, mixed_arrived[0]) for item in rows_of]
+
+    part_down = sum(
+        jnp.einsum("tef,td->efd", a, b, preferred_element_type=jnp.float32)
+        for a, b in zip(weights_of, cots)
+    ).astype(jnp.bfloat16)
+    part_up = sum(
+        jnp.einsum("td,tef->edf", a, b, preferred_element_type=jnp.float32)
+        for a, b in zip(rows_of, grad_pres)
+    ).astype(jnp.bfloat16)
+    down_sum = reduce_dp(part_down, 2)
+    up_sum = reduce_dp(part_up, 1)
+
+    mixed = (tokens.astype(jnp.float32) + mixed_sum).astype(jnp.bfloat16)
+    token_grad = (cotangent.astype(jnp.float32) + grad_sum).astype(jnp.bfloat16)
+    return (mixed, token_grad, up_sum, down_sum)
+
+
+def per_device_wide(tokens, routes, gates, cotangent, w_up, w_down):
+    n_expert = lax.axis_size("expert")
+    local_experts, model_width, _ = w_up.shape
+    experts_all = local_experts * n_expert
+    tok_rows = tokens.shape[0]
+    top_k = routes.shape[1]
+    capacity = tok_rows * top_k // experts_all
 
     gate_full = kept_gates(routes, gates, experts_all, capacity)
     gate_hi = gate_full.astype(jnp.bfloat16)
@@ -87,8 +260,9 @@
 
 
 def solution(mesh):
+    small = mesh.shape["expert"] <= 8
     return jax.shard_map(
-        per_device,
+        per_device if small else per_device_wide,
         mesh=mesh,
         in_specs=(
             P(("expert", "dp"), None),

time: 462 us -> 312 us (0.68)
  waiting for transfers between devices: 382 us -> 176 us
  starting transfers between devices: 0.42 us -> 59.6 us
  other arithmetic: 6.98 us -> 26.2 us
  matrix products: 54.6 us -> 38.9 us
  between operations: 14.2 us -> 1.18 us
  local copies, waits for them, and re-layouts: 3.58 us -> 9.58 us
    reduce_scatter x4 -> x0, waiting for transfers between devices: 238 us -> none  [the longest x1 89.6 us: per_device(): lax.psum_scatter(mixed_part, 'expert', scatter_dimension=0, tiled=True)]
    ppermute x0 -> x34, waiting for transfers between devices: none -> 176 us  [shifted(): return lax.ppermute(value, axis, table)]
    all_gather x2 -> x0, waiting for transfers between devices: 143 us -> none  [the longest x1 73.7 us: per_device(): all_tokens = lax.all_gather(tokens, 'expert', axis=0, tiled=True)]
    ppermute x0 -> x34, starting transfers between devices: none -> 59.6 us  [shifted(): return lax.ppermute(value, axis, table)]
    convert_element_type x2 -> x12, other arithmetic: 3.93 us -> 20.4 us  [the longest x6 8.53 us: scatter(): column = total(sz, *arrived[-1:]).astype(jnp.bfloat16)]
    dot_general x4 -> x8, matrix products: 36.8 us -> 28.9 us  [the longest x2 10.9 us: per_device(): jnp.einsum('td,efd->tef', rows, w_down, preferred_element_type=jnp.float32)]
    dot_general x1 -> x2, matrix products: 9.34 us -> 5.06 us  [per_device(): jnp.einsum('tef,efd->td', weighted, w_down, preferred_element_type=jnp.fl...]
  transfers between devices with their start and end apart: 6 -> 34, of which waited for: 6 -> 15; matrix products, arithmetic and copies ran while one was open for 10% -> 18% of each run, Pallas kernels for 0% -> 0%
where the time goes in v2:
time: 312 us
  waiting for transfers between devices  176 us (56%)
  starting transfers between devices  59.6 us (19%)
  matrix products  38.9 us (12%)
  other arithmetic  26.2 us (8%)
  local copies, waits for them, and re-layouts  9.58 us (3%)
    ppermute x34, waiting for transfers between devices, shifted(): return lax.ppermute(value, axis, table)  176 us
    ppermute x34, starting transfers between devices, shifted(): return lax.ppermute(value, axis, table)  59.6 us
    dot_general x2, matrix products, per_device(): jnp.einsum('td,efd->tef', rows, w_down, preferred_element_type=jnp.float32)  10.9 us
    convert_element_type x6, other arithmetic, scatter(): column = total(sz, *arrived[-1:]).astype(jnp.bfloat16)  8.53 us
    dot_general x2, matrix products, per_device(): jnp.einsum('tef,td->efd', a, b, preferred_element_type=jnp.float32)  7.47 us
    unnamed x53, local copies, waits for them, and re-layouts  6.52 us
  transfers between devices with their start and end apart: 34, of which 15 were waited for; matrix products, arithmetic and copies ran while one was open for 18% of the time, Pallas kernels for 0%

profile of v2, /device:TPU:0, one launch (start us, length us, event | category | flops | bytes accessed | tf_op | source)
XLA Modules:
  0.0 311.8 jit_solution(16205858701731472470)
XLA Ops:
  3.8 3.0 collective-permute-start.2
  6.8 3.6 %collective-permute-start.5 = (bf16[128,2176]{0,1:T(8,128)(2,1)S(1)}, bf16[128,2176]{0,1:T(8,128)(2,1)S(1)}, u32[]{:S(2)}, u32[]{:S(2)}) collective-permute-start(bf16[128,2176]{0,1:T(8,128)(2,1)S(1)} %pad_maximum_fusion.1), channel_id=1, source_target_pairs={{0,24},{4,28},{8,0},{12,4},{16,8},{20,12},{24,16},{28,20},{1,25},{... | collective-permute-start | bytes 1671176 | tf_op jit(solution)/shard_map/ppermute | solution.py:32
  11.4 8.0 %collective-permute-done.2 = bf16[128,2176]{0,1:T(8,128)(2,1)S(1)} collective-permute-done((bf16[128,2176]{0,1:T(8,128)(2,1)S(1)}, bf16[128,2176]{0,1:T(8,128)(2,1)S(1)}, u32[]{:S(2)}, u32[]{:S(2)}) %collective-permute-start.2) | collective-permute-done | bytes 557088 | tf_op jit(solution)/shard_map/ppermute | solution.py:32
  19.4 1.7 collective-permute-start.3
  21.2 2.2 collective-permute-done.5
  23.4 12.9 %collective-permute-done = bf16[128,2176]{0,1:T(8,128)(2,1)S(1)} collective-permute-done((bf16[128,2176]{0,1:T(8,128)(2,1)S(1)}, bf16[128,2176]{0,1:T(8,128)(2,1)S(1)}, u32[]{:S(2)}, u32[]{:S(2)}) %collective-permute-start) | collective-permute-done | bytes 557088 | tf_op jit(solution)/shard_map/ppermute | solution.py:32
  36.4 1.5 collective-permute-start.18
  37.9 8.9 %collective-permute-start.15 = (bf16[128,2048]{1,0:T(8,128)(2,1)S(1)}, bf16[128,2048]{1,0:T(8,128)(2,1)}, u32[]{:S(2)}, u32[]{:S(2)}) collective-permute-start(bf16[128,2048]{1,0:T(8,128)(2,1)S(1)} %copy-done.8), channel_id=1, source_target_pairs={{0,8},{4,12},{8,16},{12,20},{16,24},{20,28},{24,0},{28,4},{1,9},{5... | collective-permute-start | bytes 1572872 | tf_op jit(solution)/shard_map/ppermute | solution.py:32
  47.4 23.2 %collective-permute-done.1 = bf16[128,2176]{0,1:T(8,128)(2,1)} collective-permute-done((bf16[128,2176]{0,1:T(8,128)(2,1)S(1)}, bf16[128,2176]{0,1:T(8,128)(2,1)}, u32[]{:S(2)}, u32[]{:S(2)}) %collective-permute-start.1) | collective-permute-done | bytes 557088 | tf_op jit(solution)/shard_map/ppermute | solution.py:32
  70.5 4.2 %collective-permute-done.18 = bf16[128,2048]{1,0:T(8,128)(2,1)} collective-permute-done((bf16[128,2048]{1,0:T(8,128)(2,1)S(1)}, bf16[128,2048]{1,0:T(8,128)(2,1)}, u32[]{:S(2)}, u32[]{:S(2)}) %collective-permute-start.18) | collective-permute-done | bytes 524320 | tf_op jit(solution)/shard_map/ppermute | solution.py:32
  77.3 25.5 %collective-permute-done.16 = bf16[128,2048]{1,0:T(8,128)(2,1)} collective-permute-done((bf16[128,2048]{1,0:T(8,128)(2,1)S(1)}, bf16[128,2048]{1,0:T(8,128)(2,1)}, u32[]{:S(2)}, u32[]{:S(2)}) %collective-permute-start.16) | collective-permute-done | bytes 524320 | tf_op jit(solution)/shard_map/ppermute | solution.py:32
  105.0 4.2 %pad_maximum_fusion = bf16[512,2176]{0,1:T(8,128)(2,1)S(1)} fusion(bf16[128,2176]{0,1:T(8,128)(2,1)} %copy-done.14, bf16[128,2176]{0,1:T(8,128)(2,1)} %collective-permute-done.1, bf16[128,2176]{0,1:T(8,128)(2,1)} %copy-done.15, bf16[128,64]{0,1:T(8,128)(2,1)S(1)} %get-tuple-element.48, bf16[128,64]{0,1:T(8,128)(2,1)S(1)} %get-tuple-element.49, ...), kind=kLoop, calls=%fused_computation.6 | loop fusion | flops 13369344 | bytes 4456448 | tf_op jit(solution)/shard_map/concatenate | solution.py:90
  109.3 9.3 %collective-permute-done.7 = bf16[128,2176]{0,1:T(8,128)(2,1)S(1)} collective-permute-done((bf16[128,2176]{0,1:T(8,128)(2,1)}, bf16[128,2176]{0,1:T(8,128)(2,1)S(1)}, u32[]{:S(2)}, u32[]{:S(2)}) %collective-permute-start.7) | collective-permute-done | bytes 557088 | tf_op jit(solution)/shard_map/ppermute | solution.py:32
  118.8 2.9 multiply_convert_fusion.3
  121.7 2.9 multiply_convert_fusion.2
  124.6 2.8 collective-permute-done.20
  127.5 5.6 %multiply_convert_fusion = bf16[512,8,128]{2,0,1:T(8,128)(2,1)S(1)} fusion(f32[512,8,128]{2,0,1:T(8,128)S(1)} %get-tuple-element.63, bf16[8,128,2048]{2,1,0:T(8,128)(2,1)S(1)} %copy-done.19, f32[512,8]{0,1:T(8,128)S(1)} %get-tuple-element.66, bf16[128,2048]{1,0:T(8,128)(2,1)} %collective-permute-done.19, bf16[128,2048]{1,0:T(8,128)(2,1)S(1)} %collective-permute-done.20, ...), kind=kOutput, calls=%fused_computation.23 | convolution fusion | flops 2165833728 | bytes 9453568 | tf_op jit(solution)/shard_map/td,efd->tef/dot_general | solution.py:175
  134.1 2.4 bitcast_convert_fusion
  140.2 2.5 bitcast_convert_fusion.2
  143.9 1.5 collective-permute-start.8
  145.9 5.2 %multiply_convert_fusion.1 = bf16[512,8,128]{2,0,1:T(8,128)(2,1)S(1)} fusion(f32[512,8,128]{2,0,1:T(8,128)S(1)} %get-tuple-element.65, bf16[8,128,2048]{2,1,0:T(8,128)(2,1)S(1)} %copy-done.19, f32[512,8]{0,1:T(8,128)S(1)} %get-tuple-element.67, bf16[128,2048]{1,0:T(8,128)(2,1)} %collective-permute-done.18, bf16[128,2048]{1,0:T(8,128)(2,1)} %collective-permute-done.16, ...), kind=kOutput, calls=%fused_computation.24 | convolution fusion | flops 2165833728 | bytes 9453568 | tf_op jit(solution)/shard_map/td,efd->tef/dot_general | solution.py:175
  151.2 2.4 bitcast_convert_fusion.1
  153.6 21.3 %collective-permute-done.22 = bf16[128,2048]{1,0:T(8,128)(2,1)S(1)} collective-permute-done((bf16[128,2048]{1,0:T(8,128)(2,1)S(1)}, bf16[128,2048]{1,0:T(8,128)(2,1)S(1)}, u32[]{:S(2)}, u32[]{:S(2)}) %collective-permute-start.22) | collective-permute-done | bytes 524320 | tf_op jit(solution)/shard_map/ppermute | solution.py:32
  175.8 3.1 collective-permute-start.23
  178.9 2.5 bitcast_convert_fusion.3
  181.4 12.8 %collective-permute-done.9 = bf16[128,2048]{1,0:T(8,128)(2,1)S(1)} collective-permute-done((bf16[128,2048]{1,0:T(8,128)(2,1)S(1)}, bf16[128,2048]{1,0:T(8,128)(2,1)S(1)}, u32[]{:S(2)}, u32[]{:S(2)}) %collective-permute-start.9) | collective-permute-done | bytes 524320 | tf_op jit(solution)/shard_map/ppermute | solution.py:32
  195.2 6.8 %collective-permute-start.10 = (bf16[128,2048]{1,0:T(8,128)(2,1)}, bf16[128,2048]{1,0:T(8,128)(2,1)}, u32[]{:S(2)}, u32[]{:S(2)}) collective-permute-start(bf16[128,2048]{1,0:T(8,128)(2,1)} %add_convert_fusion.11), channel_id=1, source_target_pairs={{0,24},{4,28},{8,0},{12,4},{16,8},{20,12},{24,16},{28,20},{1,25},{... | collective-permute-start | bytes 1572872 | tf_op jit(solution)/shard_map/ppermute | solution.py:32
  202.5 1.6 copy-done.3
  204.3 1.6 collective-permute-start.26
  207.8 2.0 add_convert_fusion.6
  209.8 9.9 %collective-permute-start.25 = (bf16[128,2048]{1,0:T(8,128)(2,1)}, bf16[128,2048]{1,0:T(8,128)(2,1)}, u32[]{:S(2)}, u32[]{:S(2)}) collective-permute-start(bf16[128,2048]{1,0:T(8,128)(2,1)} %add_convert_fusion.6), channel_id=1, source_target_pairs={{0,8},{4,12},{8,16},{12,20},{16,24},{20,28},{24,0},{28,4},{1,9},{5... | collective-permute-start | bytes 1572872 | tf_op jit(solution)/shard_map/ppermute | solution.py:32
  219.7 7.3 %collective-permute-done.10 = bf16[128,2048]{1,0:T(8,128)(2,1)} collective-permute-done((bf16[128,2048]{1,0:T(8,128)(2,1)}, bf16[128,2048]{1,0:T(8,128)(2,1)}, u32[]{:S(2)}, u32[]{:S(2)}) %collective-permute-start.10) | collective-permute-done | bytes 524320 | tf_op jit(solution)/shard_map/ppermute | solution.py:32
  227.1 2.0 add_convert_fusion.10
  229.9 2.4 fusion.3
  232.3 2.4 add_convert_fusion.1
  235.9 3.7 %fusion.12 = f32[8,128,2048]{2,1,0:T(8,128)S(1)} fusion(bf16[512,8,128]{2,0,1:T(8,128)(2,1)S(1)} %copy-done.11, bf16[128,2048]{1,0:T(8,128)(2,1)} %collective-permute-done.18, bf16[128,2048]{1,0:T(8,128)(2,1)} %collective-permute-done.16, bf16[128,2048]{1,0:T(8,128)(2,1)} %collective-permute-done.15, bf16[128,2048]{1,0:T(8,128)(2,1)S(1)} %copy-done.8), kind=kOutput, calls=%fused_computation.42 | convolution fusion | flops 2155872256 | bytes 11534336 | tf_op jit(solution)/shard_map/tef,td->efd/dot_general | solution.py:190
  239.7 3.7 %add_convert_fusion = bf16[8,128,2048]{2,1,0:T(8,128)(2,1)S(1)} fusion(f32[8,128,2048]{2,1,0:T(8,128)S(1)} %fusion.12, bf16[512,8,128]{2,0,1:T(8,128)(2,1)S(1)} %copy-done.13, bf16[128,2048]{1,0:T(8,128)(2,1)} %collective-permute-done.19, bf16[128,2048]{1,0:T(8,128)(2,1)S(1)} %copy-done.17, bf16[128,2048]{1,0:T(8,128)(2,1)} %collective-permute-done.17, ...), kind=kOutput, calls=%fused_computation | convolution fusion | flops 2160066560 | bytes 15728640 | tf_op jit(solution)/shard_map/tef,td->efd/dot_general | solution.py:190
  244.3 1.6 add_convert_fusion.5
  245.9 2.1 collective-permute-start.27
  250.2 1.6 fusion
  251.8 1.6 collective-permute-start.30
  254.7 29.4 %collective-permute-done.27 = bf16[128,2048]{1,0:T(8,128)(2,1)S(1)} collective-permute-done((bf16[128,2048]{1,0:T(8,128)(2,1)S(1)}, bf16[128,2048]{1,0:T(8,128)(2,1)S(1)}, u32[]{:S(2)}, u32[]{:S(2)}) %collective-permute-start.27) | collective-permute-done | bytes 524320 | tf_op jit(solution)/shard_map/ppermute | solution.py:32
  284.1 1.5 collective-permute-start.33
  285.7 2.5 add_convert_fusion.4
  288.2 6.7 %collective-permute-done.14 = bf16[128,2048]{1,0:T(8,128)(2,1)S(1)} collective-permute-done((bf16[128,2048]{1,0:T(8,128)(2,1)S(1)}, bf16[128,2048]{1,0:T(8,128)(2,1)S(1)}, u32[]{:S(2)}, u32[]{:S(2)}) %collective-permute-start.14) | collective-permute-done | bytes 524320 | tf_op jit(solution)/shard_map/ppermute | solution.py:32
  294.8 2.7 add_convert_fusion.8
  299.4 9.2 %collective-permute-done.33 = bf16[8,128,512]{2,1,0:T(8,128)(2,1)} collective-permute-done((bf16[8,128,512]{2,1,0:T(8,128)(2,1)}, bf16[8,128,512]{2,1,0:T(8,128)(2,1)}, u32[]{:S(2)}, u32[]{:S(2)}) %collective-permute-start.33) | collective-permute-done | bytes 1048608 | tf_op jit(solution)/shard_map/ppermute | solution.py:32
  308.5 3.3 %add_convert_fusion.2 = bf16[8,128,512]{2,1,0:T(8,128)(2,1)} fusion(bf16[8,128,512]{2,1,0:T(8,128)(2,1)} %collective-permute-done.33, bf16[8,128,512]{2,1,0:T(8,128)(2,1)} %collective-permute-done.31, bf16[8,128,2048]{2,1,0:T(8,128)(2,1)} %copy-done, s32[]{:T(128)S(6)} %select_n.70), kind=kLoop, calls=%fused_computation.21 | loop fusion | flops 3145728 | bytes 4194308 | tf_op jit(solution)/shard_map/convert_element_type | solution.py:139
  (112 shorter events, 28.9 us)
Async XLA Ops:
  0.6 18.8 %copy-start.8 = (bf16[128,2048]{1,0:T(8,128)(2,1)S(1)}, bf16[128,2048]{1,0:T(8,128)(2,1)}, u32[]{:S(2)}) copy-start(bf16[128,2048]{1,0:T(8,128)(2,1)} %param.9) | copy-start | bytes 1572868
  3.8 15.7 %collective-permute-start.2 = (bf16[128,2176]{0,1:T(8,128)(2,1)S(1)}, bf16[128,2176]{0,1:T(8,128)(2,1)S(1)}, u32[]{:S(2)}, u32[]{:S(2)}) collective-permute-start(bf16[128,2176]{0,1:T(8,128)(2,1)S(1)} %pad_maximum_fusion.1), channel_id=1, source_target_pairs={{0,4},{4,0},{8,12},{12,8},{16,20},{20,16},{24,28},{28,24},{1,5},{5... | collective-permute-start | bytes 1671176 | tf_op jit(solution)/shard_map/ppermute | solution.py:32
  6.8 16.6 %collective-permute-start.5 = (bf16[128,2176]{0,1:T(8,128)(2,1)S(1)}, bf16[128,2176]{0,1:T(8,128)(2,1)S(1)}, u32[]{:S(2)}, u32[]{:S(2)}) collective-permute-start(bf16[128,2176]{0,1:T(8,128)(2,1)S(1)} %pad_maximum_fusion.1), channel_id=1, source_target_pairs={{0,24},{4,28},{8,0},{12,4},{16,8},{20,12},{24,16},{28,20},{1,25},{... | collective-permute-start | bytes 1671176 | tf_op jit(solution)/shard_map/ppermute | solution.py:32
  10.4 26.0 %collective-permute-start = (bf16[128,2176]{0,1:T(8,128)(2,1)S(1)}, bf16[128,2176]{0,1:T(8,128)(2,1)S(1)}, u32[]{:S(2)}, u32[]{:S(2)}) collective-permute-start(bf16[128,2176]{0,1:T(8,128)(2,1)S(1)} %pad_maximum_fusion.1), channel_id=1, source_target_pairs={{0,8},{4,12},{8,16},{12,20},{16,24},{20,28},{24,0},{28,4},{1,9},{5... | collective-permute-start | bytes 1671176 | tf_op jit(solution)/shard_map/ppermute | solution.py:32
  10.4 60.1 %collective-permute-start.1 = (bf16[128,2176]{0,1:T(8,128)(2,1)S(1)}, bf16[128,2176]{0,1:T(8,128)(2,1)}, u32[]{:S(2)}, u32[]{:S(2)}) collective-permute-start(bf16[128,2176]{0,1:T(8,128)(2,1)S(1)} %pad_maximum_fusion.1), channel_id=1, source_target_pairs={{0,16},{4,20},{8,24},{12,28},{16,0},{20,4},{24,8},{28,12},{1,17},{... | collective-permute-start | bytes 1671176 | tf_op jit(solution)/shard_map/ppermute | solution.py:32
  19.4 27.4 %collective-permute-start.3 = (bf16[128,2048]{1,0:T(8,128)(2,1)S(1)}, bf16[128,2048]{1,0:T(8,128)(2,1)}, u32[]{:S(2)}, u32[]{:S(2)}) collective-permute-start(bf16[128,2048]{1,0:T(8,128)(2,1)S(1)} %copy-done.8), channel_id=1, source_target_pairs={{0,4},{4,0},{8,12},{12,8},{16,20},{20,16},{24,28},{28,24},{1,5},{5... | collective-permute-start | bytes 1572872 | tf_op jit(solution)/shard_map/ppermute | solution.py:32
  23.4 81.6 %copy-start.14 = (bf16[128,2176]{0,1:T(8,128)(2,1)}, bf16[128,2176]{0,1:T(8,128)(2,1)S(1)}, u32[]{:S(2)}) copy-start(bf16[128,2176]{0,1:T(8,128)(2,1)S(1)} %collective-permute-done.5) | copy-start | bytes 1671172
  36.4 68.6 %copy-start.15 = (bf16[128,2176]{0,1:T(8,128)(2,1)}, bf16[128,2176]{0,1:T(8,128)(2,1)S(1)}, u32[]{:S(2)}) copy-start(bf16[128,2176]{0,1:T(8,128)(2,1)S(1)} %collective-permute-done) | copy-start | bytes 1671172
  36.4 38.3 %collective-permute-start.18 = (bf16[128,2048]{1,0:T(8,128)(2,1)S(1)}, bf16[128,2048]{1,0:T(8,128)(2,1)}, u32[]{:S(2)}, u32[]{:S(2)}) collective-permute-start(bf16[128,2048]{1,0:T(8,128)(2,1)S(1)} %copy-done.8), channel_id=1, source_target_pairs={{0,24},{4,28},{8,0},{12,4},{16,8},{20,12},{24,16},{28,20},{1,25},{... | collective-permute-start | bytes 1572872 | tf_op jit(solution)/shard_map/ppermute | solution.py:32
  37.9 37.3 %collective-permute-start.15 = (bf16[128,2048]{1,0:T(8,128)(2,1)S(1)}, bf16[128,2048]{1,0:T(8,128)(2,1)}, u32[]{:S(2)}, u32[]{:S(2)}) collective-permute-start(bf16[128,2048]{1,0:T(8,128)(2,1)S(1)} %copy-done.8), channel_id=1, source_target_pairs={{0,8},{4,12},{8,16},{12,20},{16,24},{20,28},{24,0},{28,4},{1,9},{5... | collective-permute-start | bytes 1572872 | tf_op jit(solution)/shard_map/ppermute | solution.py:32
  46.8 58.0 %collective-permute-start.4 = (bf16[128,2176]{0,1:T(8,128)(2,1)S(1)}, bf16[128,2176]{0,1:T(8,128)(2,1)S(1)}, u32[]{:S(2)}, u32[]{:S(2)}) collective-permute-start(bf16[128,2176]{0,1:T(8,128)(2,1)S(1)} %collective-permute-done), channel_id=1, source_target_pairs={{0,4},{4,0},{8,12},{12,8},{16,20},{20,16},{24,28},{28,24},{1,5},{5... | collective-permute-start | bytes 1671176 | tf_op jit(solution)/shard_map/ppermute | solution.py:32
  70.5 32.3 %collective-permute-start.16 = (bf16[128,2048]{1,0:T(8,128)(2,1)S(1)}, bf16[128,2048]{1,0:T(8,128)(2,1)}, u32[]{:S(2)}, u32[]{:S(2)}) collective-permute-start(bf16[128,2048]{1,0:T(8,128)(2,1)S(1)} %copy-done.8), channel_id=1, source_target_pairs={{0,16},{4,20},{8,24},{12,28},{16,0},{20,4},{24,8},{28,12},{1,17},{... | collective-permute-start | bytes 1572872 | tf_op jit(solution)/shard_map/ppermute | solution.py:32
  74.7 28.7 %collective-permute-start.19 = (bf16[128,2048]{1,0:T(8,128)(2,1)}, bf16[128,2048]{1,0:T(8,128)(2,1)}, u32[]{:S(2)}, u32[]{:S(2)}) collective-permute-start(bf16[128,2048]{1,0:T(8,128)(2,1)} %collective-permute-done.18), channel_id=1, source_target_pairs={{0,4},{4,0},{8,12},{12,8},{16,20},{20,16},{24,28},{28,24},{1,5},{5... | collective-permute-start | bytes 1572872 | tf_op jit(solution)/shard_map/ppermute | solution.py:32
  75.2 29.6 %collective-permute-start.17 = (bf16[128,2048]{1,0:T(8,128)(2,1)}, bf16[128,2048]{1,0:T(8,128)(2,1)}, u32[]{:S(2)}, u32[]{:S(2)}) collective-permute-start(bf16[128,2048]{1,0:T(8,128)(2,1)} %collective-permute-done.15), channel_id=1, source_target_pairs={{0,4},{4,0},{8,12},{12,8},{16,20},{20,16},{24,28},{28,24},{1,5},{5... | collective-permute-start | bytes 1572872 | tf_op jit(solution)/shard_map/ppermute | solution.py:32
  76.7 28.3 %collective-permute-start.6 = (bf16[128,2176]{0,1:T(8,128)(2,1)S(1)}, bf16[128,2176]{0,1:T(8,128)(2,1)S(1)}, u32[]{:S(2)}, u32[]{:S(2)}) collective-permute-start(bf16[128,2176]{0,1:T(8,128)(2,1)S(1)} %collective-permute-done.5), channel_id=1, source_target_pairs={{0,4},{4,0},{8,12},{12,8},{16,20},{20,16},{24,28},{28,24},{1,5},{5... | collective-permute-start | bytes 1671176 | tf_op jit(solution)/shard_map/ppermute | solution.py:32
  102.8 15.7 %collective-permute-start.7 = (bf16[128,2176]{0,1:T(8,128)(2,1)}, bf16[128,2176]{0,1:T(8,128)(2,1)S(1)}, u32[]{:S(2)}, u32[]{:S(2)}) collective-permute-start(bf16[128,2176]{0,1:T(8,128)(2,1)} %collective-permute-done.1), channel_id=1, source_target_pairs={{0,4},{4,0},{8,12},{12,8},{16,20},{20,16},{24,28},{28,24},{1,5},{5... | collective-permute-start | bytes 1671176 | tf_op jit(solution)/shard_map/ppermute | solution.py:32
  103.4 24.1 %collective-permute-start.20 = (bf16[128,2048]{1,0:T(8,128)(2,1)}, bf16[128,2048]{1,0:T(8,128)(2,1)S(1)}, u32[]{:S(2)}, u32[]{:S(2)}) collective-permute-start(bf16[128,2048]{1,0:T(8,128)(2,1)} %collective-permute-done.16), channel_id=1, source_target_pairs={{0,4},{4,0},{8,12},{12,8},{16,20},{20,16},{24,28},{28,24},{1,5},{5... | collective-permute-start | bytes 1572872 | tf_op jit(solution)/shard_map/ppermute | solution.py:32
  105.0 13.8 %copy-start.18 = (bf16[8,2048,128]{2,1,0:T(8,128)(2,1)S(1)}, bf16[8,2048,128]{2,1,0:T(8,128)(2,1)}, u32[]{:S(2)}) copy-start(bf16[8,2048,128]{2,1,0:T(8,128)(2,1)} %param.10) | copy-start | bytes 12582916
  109.3 93.3 %copy-start.1 = (bf16[512,2176]{0,1:T(8,128)(2,1)}, bf16[512,2176]{0,1:T(8,128)(2,1)S(1)}, u32[]{:S(2)}) copy-start(bf16[512,2176]{0,1:T(8,128)(2,1)S(1)} %pad_maximum_fusion) | copy-start | bytes 6684676
  121.7 57.2 %copy-start.10 = (bf16[512,8,128]{2,0,1:T(8,128)(2,1)}, bf16[512,8,128]{2,0,1:T(8,128)(2,1)S(1)}, u32[]{:S(2)}) copy-start(bf16[512,8,128]{2,0,1:T(8,128)(2,1)S(1)} %get-tuple-element.34) | copy-start | bytes 3145732
  121.7 5.8 %copy-start.19 = (bf16[8,128,2048]{2,1,0:T(8,128)(2,1)S(1)}, bf16[8,128,2048]{2,1,0:T(8,128)(2,1)}, u32[]{:S(2)}) copy-start(bf16[8,128,2048]{2,1,0:T(8,128)(2,1)} %param.11) | copy-start | bytes 12582916
  124.6 15.5 %copy-start.12 = (bf16[512,8,128]{2,0,1:T(8,128)(2,1)}, bf16[512,8,128]{2,0,1:T(8,128)(2,1)S(1)}, u32[]{:S(2)}) copy-start(bf16[512,8,128]{2,0,1:T(8,128)(2,1)S(1)} %get-tuple-element.35) | copy-start | bytes 3145732
  137.6 64.4 %collective-permute-start.21 = (bf16[128,2048]{1,0:T(8,128)(2,1)S(1)}, bf16[128,2048]{1,0:T(8,128)(2,1)S(1)}, u32[]{:S(2)}, u32[]{:S(2)}) collective-permute-start(bf16[128,2048]{1,0:T(8,128)(2,1)S(1)} %get-tuple-element.54), channel_id=1, source_target_pairs={{0,4},{4,0},{8,12},{12,8},{16,20},{20,16},{24,28},{28,24},{1,5},{5... | collective-permute-start | bytes 1572872 | tf_op jit(solution)/shard_map/ppermute | solution.py:32
  138.1 67.8 %collective-permute-start.24 = (bf16[128,2048]{1,0:T(8,128)(2,1)}, bf16[128,2048]{1,0:T(8,128)(2,1)}, u32[]{:S(2)}, u32[]{:S(2)}) collective-permute-start(bf16[128,2048]{1,0:T(8,128)(2,1)} %get-tuple-element.56), channel_id=1, source_target_pairs={{0,4},{4,0},{8,12},{12,8},{16,20},{20,16},{24,28},{28,24},{1,5},{5... | collective-permute-start | bytes 1572872 | tf_op jit(solution)/shard_map/ppermute | solution.py:32
  139.6 35.2 %collective-permute-start.22 = (bf16[128,2048]{1,0:T(8,128)(2,1)S(1)}, bf16[128,2048]{1,0:T(8,128)(2,1)S(1)}, u32[]{:S(2)}, u32[]{:S(2)}) collective-permute-start(bf16[128,2048]{1,0:T(8,128)(2,1)S(1)} %get-tuple-element.57), channel_id=1, source_target_pairs={{0,4},{4,0},{8,12},{12,8},{16,20},{20,16},{24,28},{28,24},{1,5},{5... | collective-permute-start | bytes 1572872 | tf_op jit(solution)/shard_map/ppermute | solution.py:32
  143.9 60.5 %collective-permute-start.8 = (bf16[128,2048]{1,0:T(8,128)(2,1)}, bf16[128,2048]{1,0:T(8,128)(2,1)}, u32[]{:S(2)}, u32[]{:S(2)}) collective-permute-start(bf16[128,2048]{1,0:T(8,128)(2,1)} %get-tuple-element.58), channel_id=1, source_target_pairs={{0,4},{4,0},{8,12},{12,8},{16,20},{20,16},{24,28},{28,24},{1,5},{5... | collective-permute-start | bytes 1572872 | tf_op jit(solution)/shard_map/ppermute | solution.py:32
  145.4 48.8 %collective-permute-start.9 = (bf16[128,2048]{1,0:T(8,128)(2,1)S(1)}, bf16[128,2048]{1,0:T(8,128)(2,1)S(1)}, u32[]{:S(2)}, u32[]{:S(2)}) collective-permute-start(bf16[128,2048]{1,0:T(8,128)(2,1)S(1)} %get-tuple-element.61), channel_id=1, source_target_pairs={{0,4},{4,0},{8,12},{12,8},{16,20},{20,16},{24,28},{28,24},{1,5},{5... | collective-permute-start | bytes 1572872 | tf_op jit(solution)/shard_map/ppermute | solution.py:32
  153.5 27.8 %copy-start.4 = (bf16[512,2048]{1,0:T(8,128)(2,1)}, bf16[512,2048]{1,0:T(8,128)(2,1)S(1)}, u32[]{:S(2)}) copy-start(bf16[512,2048]{1,0:T(8,128)(2,1)S(1)} %bitcast_convert_fusion.1) | copy-start | bytes 6291460
  175.8 32.1 %collective-permute-start.23 = (bf16[128,2048]{1,0:T(8,128)(2,1)}, bf16[128,2048]{1,0:T(8,128)(2,1)}, u32[]{:S(2)}, u32[]{:S(2)}) collective-permute-start(bf16[128,2048]{1,0:T(8,128)(2,1)} %add_convert_fusion.7), channel_id=1, source_target_pairs={{0,24},{4,28},{8,0},{12,4},{16,8},{20,12},{24,16},{28,20},{1,25},{... | collective-permute-start | bytes 1572872 | tf_op jit(solution)/shard_map/ppermute | solution.py:32
  181.4 12.8 %copy-start.6 = (bf16[512,2048]{1,0:T(8,128)(2,1)}, bf16[512,2048]{1,0:T(8,128)(2,1)S(1)}, u32[]{:S(2)}) copy-start(bf16[512,2048]{1,0:T(8,128)(2,1)S(1)} %bitcast_convert_fusion.3) | copy-start | bytes 6291460
  195.2 31.9 %collective-permute-start.10 = (bf16[128,2048]{1,0:T(8,128)(2,1)}, bf16[128,2048]{1,0:T(8,128)(2,1)}, u32[]{:S(2)}, u32[]{:S(2)}) collective-permute-start(bf16[128,2048]{1,0:T(8,128)(2,1)} %add_convert_fusion.11), channel_id=1, source_target_pairs={{0,24},{4,28},{8,0},{12,4},{16,8},{20,12},{24,16},{28,20},{1,25},{... | collective-permute-start | bytes 1572872 | tf_op jit(solution)/shard_map/ppermute | solution.py:32
  202.0 25.1 %collective-permute-start.11 = (bf16[128,2048]{1,0:T(8,128)(2,1)}, bf16[128,2048]{1,0:T(8,128)(2,1)}, u32[]{:S(2)}, u32[]{:S(2)}) collective-permute-start(bf16[128,2048]{1,0:T(8,128)(2,1)} %get-tuple-element.60), channel_id=1, source_target_pairs={{0,4},{4,0},{8,12},{12,8},{16,20},{20,16},{24,28},{28,24},{1,5},{5... | collective-permute-start | bytes 1572872 | tf_op jit(solution)/shard_map/ppermute | solution.py:32
  204.2 22.9 %copy-start.7 = (bf16[512,2048]{1,0:T(8,128)(2,1)S(1)}, bf16[512,2048]{1,0:T(8,128)(2,1)}, u32[]{:S(2)}) copy-start(bf16[512,2048]{1,0:T(8,128)(2,1)} %copy-done.6) | copy-start | bytes 6291460
  204.3 25.5 %copy-start.23 = (bf16[512,8,128]{2,0,1:T(8,128)(2,1)S(1)}, bf16[512,8,128]{2,0,1:T(8,128)(2,1)}, u32[]{:S(2)}) copy-start(bf16[512,8,128]{2,0,1:T(8,128)(2,1)} %copy-done.22) | copy-start | bytes 3145732
  204.3 39.3 %collective-permute-start.26 = (bf16[128,2048]{1,0:T(8,128)(2,1)}, bf16[128,2048]{1,0:T(8,128)(2,1)}, u32[]{:S(2)}, u32[]{:S(2)}) collective-permute-start(bf16[128,2048]{1,0:T(8,128)(2,1)} %get-tuple-element.55), channel_id=1, source_target_pairs={{0,4},{4,0},{8,12},{12,8},{16,20},{20,16},{24,28},{28,24},{1,5},{5... | collective-permute-start | bytes 1572872 | tf_op jit(solution)/shard_map/ppermute | solution.py:32
  205.9 39.9 %collective-permute-start.13 = (bf16[128,2048]{1,0:T(8,128)(2,1)}, bf16[128,2048]{1,0:T(8,128)(2,1)}, u32[]{:S(2)}, u32[]{:S(2)}) collective-permute-start(bf16[128,2048]{1,0:T(8,128)(2,1)} %get-tuple-element.59), channel_id=1, source_target_pairs={{0,4},{4,0},{8,12},{12,8},{16,20},{20,16},{24,28},{28,24},{1,5},{5... | collective-permute-start | bytes 1572872 | tf_op jit(solution)/shard_map/ppermute | solution.py:32
  209.8 33.9 %collective-permute-start.25 = (bf16[128,2048]{1,0:T(8,128)(2,1)}, bf16[128,2048]{1,0:T(8,128)(2,1)}, u32[]{:S(2)}, u32[]{:S(2)}) collective-permute-start(bf16[128,2048]{1,0:T(8,128)(2,1)} %add_convert_fusion.6), channel_id=1, source_target_pairs={{0,8},{4,12},{8,16},{12,20},{16,24},{20,28},{24,0},{28,4},{1,9},{5... | collective-permute-start | bytes 1572872 | tf_op jit(solution)/shard_map/ppermute | solution.py:32
  229.1 16.9 %collective-permute-start.12 = (bf16[128,2048]{1,0:T(8,128)(2,1)}, bf16[128,2048]{1,0:T(8,128)(2,1)}, u32[]{:S(2)}, u32[]{:S(2)}) collective-permute-start(bf16[128,2048]{1,0:T(8,128)(2,1)} %add_convert_fusion.10), channel_id=1, source_target_pairs={{0,8},{4,12},{8,16},{12,20},{16,24},{20,28},{24,0},{28,4},{1,9},{5... | collective-permute-start | bytes 1572872 | tf_op jit(solution)/shard_map/ppermute | solution.py:32
  235.0 14.2 %collective-permute-start.29 = (bf16[8,512,128]{1,2,0:T(8,128)(2,1)S(1)}, bf16[8,512,128]{1,2,0:T(8,128)(2,1)}, u32[]{:S(2)}, u32[]{:S(2)}) collective-permute-start(bf16[8,512,128]{1,2,0:T(8,128)(2,1)S(1)} %get-tuple-element.53), channel_id=1, source_target_pairs={{0,1},{1,0},{2,3},{3,2},{4,5},{5,4},{6,7},{7,6},{8,9},{9,8},{10,11... | collective-permute-start | bytes 3145736 | tf_op jit(solution)/shard_map/ppermute | solution.py:32
  243.4 10.0 %copy-start = (bf16[8,128,2048]{2,1,0:T(8,128)(2,1)}, bf16[8,128,2048]{2,1,0:T(8,128)(2,1)S(1)}, u32[]{:S(2)}) copy-start(bf16[8,128,2048]{2,1,0:T(8,128)(2,1)S(1)} %add_convert_fusion) | copy-start | bytes 12582916
  243.7 53.8 %collective-permute-start.28 = (bf16[8,512,128]{1,2,0:T(8,128)(2,1)S(1)}, bf16[8,512,128]{1,2,0:T(8,128)(2,1)S(1)}, u32[]{:S(2)}, u32[]{:S(2)}) collective-permute-start(bf16[8,512,128]{1,2,0:T(8,128)(2,1)S(1)} %get-tuple-element.52), channel_id=1, source_target_pairs={{0,1},{1,0},{2,3},{3,2},{4,5},{5,4},{6,7},{7,6},{8,9},{9,8},{10,11... | collective-permute-start | bytes 3145736 | tf_op jit(solution)/shard_map/ppermute | solution.py:32
  243.8 8.0 %collective-permute-start.32 = (bf16[8,128,512]{2,1,0:T(8,128)(2,1)S(1)}, bf16[8,128,512]{2,1,0:T(8,128)(2,1)S(1)}, u32[]{:S(2)}, u32[]{:S(2)}) collective-permute-start(bf16[8,128,512]{2,1,0:T(8,128)(2,1)S(1)} %get-tuple-element.51), channel_id=1, source_target_pairs={{0,1},{1,0},{2,3},{3,2},{4,5},{5,4},{6,7},{7,6},{8,9},{9,8},{10,11... | collective-permute-start | bytes 3145736 | tf_op jit(solution)/shard_map/ppermute | solution.py:32
  245.8 53.5 %collective-permute-start.31 = (bf16[8,128,512]{2,1,0:T(8,128)(2,1)S(1)}, bf16[8,128,512]{2,1,0:T(8,128)(2,1)}, u32[]{:S(2)}, u32[]{:S(2)}) collective-permute-start(bf16[8,128,512]{2,1,0:T(8,128)(2,1)S(1)} %get-tuple-element.50), channel_id=1, source_target_pairs={{0,1},{1,0},{2,3},{3,2},{4,5},{5,4},{6,7},{7,6},{8,9},{9,8},{10,11... | collective-permute-start | bytes 3145736 | tf_op jit(solution)/shard_map/ppermute | solution.py:32
  245.9 38.2 %collective-permute-start.27 = (bf16[128,2048]{1,0:T(8,128)(2,1)S(1)}, bf16[128,2048]{1,0:T(8,128)(2,1)S(1)}, u32[]{:S(2)}, u32[]{:S(2)}) collective-permute-start(bf16[128,2048]{1,0:T(8,128)(2,1)S(1)} %add_convert_fusion.5), channel_id=1, source_target_pairs={{0,16},{4,20},{8,24},{12,28},{16,0},{20,4},{24,8},{28,12},{1,17},{... | collective-permute-start | bytes 1572872 | tf_op jit(solution)/shard_map/ppermute | solution.py:32
  249.2 45.7 %collective-permute-start.14 = (bf16[128,2048]{1,0:T(8,128)(2,1)S(1)}, bf16[128,2048]{1,0:T(8,128)(2,1)S(1)}, u32[]{:S(2)}, u32[]{:S(2)}) collective-permute-start(bf16[128,2048]{1,0:T(8,128)(2,1)S(1)} %add_convert_fusion.9), channel_id=1, source_target_pairs={{0,16},{4,20},{8,24},{12,28},{16,0},{20,4},{24,8},{28,12},{1,17},{... | collective-permute-start | bytes 1572872 | tf_op jit(solution)/shard_map/ppermute | solution.py:32
  251.8 45.7 %collective-permute-start.30 = (bf16[8,512,128]{1,2,0:T(8,128)(2,1)S(1)}, bf16[8,512,128]{1,2,0:T(8,128)(2,1)S(1)}, u32[]{:S(2)}, u32[]{:S(2)}) collective-permute-start(bf16[8,512,128]{1,2,0:T(8,128)(2,1)S(1)} %fusion), channel_id=1, source_target_pairs={{0,2},{1,3},{2,0},{3,1},{4,6},{5,7},{6,4},{7,5},{8,10},{9,11},{10,... | collective-permute-start | bytes 3145736 | tf_op jit(solution)/shard_map/ppermute | solution.py:32
  254.7 40.1 %copy-start.9 = (bf16[128,2048]{1,0:T(8,128)(2,1)S(1)}, bf16[128,2048]{1,0:T(8,128)(2,1)}, u32[]{:S(2)}) copy-start(bf16[128,2048]{1,0:T(8,128)(2,1)} %param.6) | copy-start | bytes 1572868
  284.1 24.4 %collective-permute-start.33 = (bf16[8,128,512]{2,1,0:T(8,128)(2,1)}, bf16[8,128,512]{2,1,0:T(8,128)(2,1)}, u32[]{:S(2)}, u32[]{:S(2)}) collective-permute-start(bf16[8,128,512]{2,1,0:T(8,128)(2,1)} %add_convert_fusion.3), channel_id=1, source_target_pairs={{0,2},{1,3},{2,0},{3,1},{4,6},{5,7},{6,4},{7,5},{8,10},{9,11},{10,... | collective-permute-start | bytes 3145736 | tf_op jit(solution)/shard_map/ppermute | solution.py:32
  (11 other events, 34.2 us)

commit v3 on v2

--- a/solution.py
+++ b/solution.py
@@ -74,17 +74,17 @@
             row_of[0, by] = z_shift(rows, by)
         near, far = z_order[:-1], z_order[-1]
         for by in near:
-            cot_of[0, by] = z_shift(after(cots, *[row_of[0, b] for b in near]), by)
-        last = cot_of[n_x - 1, 0]
+            cot_of[0, by] = z_shift(after(cots, row_of[0, far]), by)
         for by in z_order:
             for sx in range(1, n_x):
-                row_of[sx, by] = x_shift(after(row_of[0, by], last), sx)
+                row_of[sx, by] = x_shift(row_of[0, by], sx)
         cot_of[0, far] = z_shift(after(cots, row_of[0, far]), far)
         for by in z_order:
             for sx in range(1, n_x):
                 cot_of[sx, by] = x_shift(cot_of[0, by], sx)
         for part in (row_of, cot_of):
             part[0, far] = after(part[0, far], *[part[n_x - 1, by] for by in near])
+        cot_of[0, 0] = after(cots, row_of[n_x - 1, far])
         return [
             [
                 jnp.concatenate([part[sx, sz] for sz in range(n_z)], axis=0)
@@ -93,7 +93,7 @@
             for part in (row_of, cot_of)
         ]
 
-    def scatter(parts):
+    def scatter(parts, name):
         def total(sz, *earlier):
             rows = slice(sz * tok_rows, (sz + 1) * tok_rows)
             value = parts[0][rows].astype(jnp.float32)
@@ -107,9 +107,9 @@
             sent[sz] = [x_shift(parts[sx][rows], -sx) for sx in range(1, n_x)]
         arrived = []
         for sz in z_order:
-            column = total(sz, *arrived[-1:]).astype(jnp.bfloat16)
+            column = total(sz, *(arrived[-1:] if name == "m" else arrived[:1])).astype(jnp.bfloat16)
             arrived.append(z_shift(column, -sz))
-        return total(0), arrived
+        return total(0, arrived[-1]), arrived
 
     def summed(own, arrived):
         for item in arrived:
@@ -167,7 +167,7 @@
         slopes.append(slope * gate_units)
         weights_of.append(weighted)
         rows_of.append(rows)
-    mixed_own, mixed_arrived = scatter(mixed_parts)
+    mixed_own, mixed_arrived = scatter(mixed_parts, "m")
     mixed_sum = summed(mixed_own, mixed_arrived)
 
     grad_pres, grad_parts = [], []
@@ -180,7 +180,7 @@
             )
         )
         grad_pres.append(grad_pre)
-    grad_own, grad_arrived = scatter(grad_parts)
+    grad_own, grad_arrived = scatter(grad_parts, "g")
     grad_sum = summed(grad_own, grad_arrived)
 
     weights_of = [after(item, mixed_arrived[0]) for item in weights_of]

time: 312 us -> 318 us (1.019)
  starting transfers between devices: 59.6 us -> 35 us
  waiting for transfers between devices: 176 us -> 197 us
  local copies, waits for them, and re-layouts: 9.58 us -> 16.1 us
  matrix products: 38.9 us -> 45.1 us
  other arithmetic: 26.2 us -> 22.9 us
    ppermute x34, starting transfers between devices: 59.6 us -> 35 us  [shifted(): return lax.ppermute(value, axis, table)]
    ppermute x34, waiting for transfers between devices: 176 us -> 197 us  [shifted(): return lax.ppermute(value, axis, table)]
    dot_general x2, matrix products: 4.78 us -> 11.5 us  [per_device(): jnp.einsum('td,tef->edf', a, b, preferred_element_type=jnp.float32)]
    convert_element_type x6 -> x5, other arithmetic: 8.53 us -> 3.84 us  [scatter(): total(sz, *(arrived[-1:] if name == 'm' else arrived[:1]))]
    unnamed x53 -> x29, local copies, waits for them, and re-layouts: 6.52 us -> 9.52 us
  transfers between devices with their start and end apart: 34 -> 34, of which waited for: 15 -> 13; matrix products, arithmetic and copies ran while one was open for 18% -> 23% of each run, Pallas kernels for 0% -> 0%
where the time goes in v3:
time: 318 us
  waiting for transfers between devices  197 us (62%)
  matrix products  45.1 us (14%)
  starting transfers between devices  35 us (11%)
  other arithmetic  22.9 us (7%)
  local copies, waits for them, and re-layouts  16.1 us (5%)
    ppermute x34, waiting for transfers between devices, shifted(): return lax.ppermute(value, axis, table)  197 us
    ppermute x34, starting transfers between devices, shifted(): return lax.ppermute(value, axis, table)  35 us
    dot_general x2, matrix products, per_device(): jnp.einsum('td,tef->edf', a, b, preferred_element_type=jnp.float32)  11.5 us
    dot_general x2, matrix products, per_device(): jnp.einsum('td,efd->tef', rows, w_down, preferred_element_type=jnp.float32)  10 us
    unnamed x29, local copies, waits for them, and re-layouts  9.52 us
    dot_general x2, matrix products, per_device(): jnp.einsum('td,edf->tef', rows, w_up, preferred_element_type=jnp.float32)  6.97 us
    dot_general x2, matrix products, per_device(): jnp.einsum('tef,td->efd', a, b, preferred_element_type=jnp.float32)  6.56 us
  transfers between devices with their start and end apart: 34, of which 13 were waited for; matrix products, arithmetic and copies ran while one was open for 23% of the time, Pallas kernels for 0%

profile of v3, /device:TPU:0, one launch (start us, length us, event | category | flops | bytes accessed | tf_op | source)
XLA Modules:
  0.0 317.6 jit_solution(2995792916502233426)
XLA Ops:
  3.8 5.1 %collective-permute-start.3 = (bf16[128,2176]{0,1:T(8,128)(2,1)S(1)}, bf16[128,2176]{0,1:T(8,128)(2,1)S(1)}, u32[]{:S(2)}, u32[]{:S(2)}) collective-permute-start(bf16[128,2176]{0,1:T(8,128)(2,1)S(1)} %pad_maximum_fusion.1), channel_id=1, source_target_pairs={{0,24},{4,28},{8,0},{12,4},{16,8},{20,12},{24,16},{28,20},{1,25},{... | collective-permute-start | bytes 1671176 | tf_op jit(solution)/shard_map/ppermute | solution.py:32
  9.9 1.5 collective-permute-start.5
  11.4 10.5 %collective-permute-done.3 = bf16[128,2176]{0,1:T(8,128)(2,1)S(1)} collective-permute-done((bf16[128,2176]{0,1:T(8,128)(2,1)S(1)}, bf16[128,2176]{0,1:T(8,128)(2,1)S(1)}, u32[]{:S(2)}, u32[]{:S(2)}) %collective-permute-start.3) | collective-permute-done | bytes 557088 | tf_op jit(solution)/shard_map/ppermute | solution.py:32
  21.9 1.5 collective-permute-start.4
  23.4 11.4 %collective-permute-done = bf16[128,2176]{0,1:T(8,128)(2,1)S(1)} collective-permute-done((bf16[128,2176]{0,1:T(8,128)(2,1)S(1)}, bf16[128,2176]{0,1:T(8,128)(2,1)S(1)}, u32[]{:S(2)}, u32[]{:S(2)}) %collective-permute-start) | collective-permute-done | bytes 557088 | tf_op jit(solution)/shard_map/ppermute | solution.py:32
  34.9 1.5 collective-permute-start.2
  36.4 20.1 %collective-permute-done.1 = bf16[128,2176]{0,1:T(8,128)(2,1)S(1)} collective-permute-done((bf16[128,2176]{0,1:T(8,128)(2,1)S(1)}, bf16[128,2176]{0,1:T(8,128)(2,1)S(1)}, u32[]{:S(2)}, u32[]{:S(2)}) %collective-permute-start.1) | collective-permute-done | bytes 557088 | tf_op jit(solution)/shard_map/ppermute | solution.py:32
  56.5 2.6 collective-permute-start.17
  60.9 10.6 %collective-permute-done.17 = bf16[128,2048]{1,0:T(8,128)(2,1)} collective-permute-done((bf16[128,2048]{1,0:T(8,128)(2,1)S(1)}, bf16[128,2048]{1,0:T(8,128)(2,1)}, u32[]{:S(2)}, u32[]{:S(2)}) %collective-permute-start.17) | collective-permute-done | bytes 524320 | tf_op jit(solution)/shard_map/ppermute | solution.py:32
  71.5 1.5 collective-permute-start.19
  73.0 29.1 %collective-permute-done.15 = bf16[128,2048]{1,0:T(8,128)(2,1)} collective-permute-done((bf16[128,2048]{1,0:T(8,128)(2,1)S(1)}, bf16[128,2048]{1,0:T(8,128)(2,1)}, u32[]{:S(2)}, u32[]{:S(2)}) %collective-permute-start.15) | collective-permute-done | bytes 524320 | tf_op jit(solution)/shard_map/ppermute | solution.py:32
  102.1 1.5 collective-permute-start.6
  104.1 1.5 collective-permute-start.20
  106.2 2.9 pad_maximum_fusion
  109.1 1.6 constant_dynamic-update-slice_fusion.2
  110.7 6.9 %collective-permute-done.6 = bf16[128,2176]{0,1:T(8,128)(2,1)S(1)} collective-permute-done((bf16[128,2176]{0,1:T(8,128)(2,1)S(1)}, bf16[128,2176]{0,1:T(8,128)(2,1)S(1)}, u32[]{:S(2)}, u32[]{:S(2)}) %collective-permute-start.6) | collective-permute-done | bytes 557088 | tf_op jit(solution)/shard_map/ppermute | solution.py:32
  119.1 2.0 copy-done.10
  121.1 4.1 %multiply_convert_fusion.3 = (bf16[512,8,128]{2,0,1:T(8,128)(2,1)S(1)}, f32[512,8,128]{2,0,1:T(8,128)}) fusion(f32[512,8]{0,1:T(8,128)S(1)} %convert_add_fusion.1, bf16[8,2048,128]{2,1,0:T(8,128)(2,1)S(1)} %copy-done.10, bf16[512,2176]{0,1:T(8,128)(2,1)S(1)} %pad_maximum_fusion), kind=kOutput, calls=%fused_computation.27 | convolution fusion | flops 2152726528 | bytes 9453568 | tf_op jit(solution)/shard_map/td,edf->tef/dot_general | solution.py:159
  125.2 2.9 multiply_convert_fusion.2
  128.1 2.5 bitcast_convert_fusion.2
  133.1 2.5 bitcast_convert_fusion.3
  136.3 15.1 %collective-permute-done.16 = bf16[128,2048]{1,0:T(8,128)(2,1)S(1)} collective-permute-done((bf16[128,2048]{1,0:T(8,128)(2,1)}, bf16[128,2048]{1,0:T(8,128)(2,1)S(1)}, u32[]{:S(2)}, u32[]{:S(2)}) %collective-permute-start.16) | collective-permute-done | bytes 524320 | tf_op jit(solution)/shard_map/ppermute | solution.py:32
  151.3 1.5 collective-permute-start.8
  152.8 4.8 %multiply_convert_fusion = bf16[512,8,128]{2,0,1:T(8,128)(2,1)S(1)} fusion(f32[512,8,128]{2,0,1:T(8,128)S(1)} %get-tuple-element.63, bf16[8,128,2048]{2,1,0:T(8,128)(2,1)S(1)} %copy-done.9, f32[512,8]{0,1:T(8,128)S(1)} %convert_add_fusion, bf16[128,2048]{1,0:T(8,128)(2,1)S(1)} %collective-permute-done.18, ...), kind=kOutput, calls=%fused_computation.23 | convolution fusion | flops 2165833728 | bytes 9453568 | tf_op jit(solution)/shard_map/td,efd->tef/dot_general | solution.py:175
  157.7 2.4 bitcast_convert_fusion
  161.8 5.2 %multiply_convert_fusion.1 = bf16[512,8,128]{2,0,1:T(8,128)(2,1)S(1)} fusion(f32[512,8,128]{2,0,1:T(8,128)S(1)} %copy-done.11, bf16[8,128,2048]{2,1,0:T(8,128)(2,1)S(1)} %copy-done.9, f32[512,8]{0,1:T(8,128)S(1)} %convert_add_fusion.1, bf16[128,2048]{1,0:T(8,128)(2,1)} %collective-permute-done.17, bf16[128,2048]{1,0:T(8,128)(2,1)} %collective-permute-done.15, ...), kind=kOutput, calls=%fused_computation.24 | convolution fusion | flops 2165833728 | bytes 9453568 | tf_op jit(solution)/shard_map/td,efd->tef/dot_general | solution.py:175
  167.2 2.4 bitcast_convert_fusion.1
  170.9 25.4 %collective-permute-done.23 = bf16[128,2048]{1,0:T(8,128)(2,1)S(1)} collective-permute-done((bf16[128,2048]{1,0:T(8,128)(2,1)S(1)}, bf16[128,2048]{1,0:T(8,128)(2,1)S(1)}, u32[]{:S(2)}, u32[]{:S(2)}) %collective-permute-start.23) | collective-permute-done | bytes 524320 | tf_op jit(solution)/shard_map/ppermute | solution.py:32
  198.0 5.7 %fusion.3 = f32[8,128,2048]{2,1,0:T(8,128)} fusion(bf16[512,8,128]{2,0,1:T(8,128)(2,1)S(1)} %multiply_convert_fusion, bf16[512,2048]{0,1:T(8,128)(2,1)S(1)} %slice.74), kind=kOutput, calls=%fused_computation.14 | convolution fusion | flops 2147483648 | bytes 11534336 | tf_op jit(solution)/shard_map/td,tef->edf/dot_general | solution.py:194
  203.7 5.8 %add_convert_fusion.1 = bf16[8,128,2048]{2,1,0:T(8,128)(2,1)S(1)} fusion(f32[8,128,2048]{2,1,0:T(8,128)} %fusion.3, bf16[512,8,128]{2,0,1:T(8,128)(2,1)S(1)} %multiply_convert_fusion.1, bf16[512,2048]{0,1:T(8,128)(2,1)S(1)} %slice-done), kind=kOutput, calls=%fused_computation.1 | convolution fusion | flops 2151677952 | bytes 15728640 | tf_op jit(solution)/shard_map/td,tef->edf/dot_general | solution.py:194
  209.5 1.7 dynamic-slice_bitcast_fusion.1
  212.1 3.7 %fusion.12 = f32[8,128,2048]{2,1,0:T(8,128)S(1)} fusion(bf16[512,8,128]{2,0,1:T(8,128)(2,1)S(1)} %get-tuple-element.32, bf16[128,2048]{1,0:T(8,128)(2,1)} %collective-permute-done.17, bf16[128,2048]{1,0:T(8,128)(2,1)} %collective-permute-done.15, bf16[128,2048]{1,0:T(8,128)(2,1)} %collective-permute-done.14, bf16[128,2048]{1,0:T(8,128)(2,1)S(1)} %copy-done.4), kind=kOutput, calls=%fused_computation.42 | convolution fusion | flops 2155872256 | bytes 11534336 | tf_op jit(solution)/shard_map/tef,td->efd/dot_general | solution.py:190
  215.8 2.8 add_convert_fusion
  219.7 1.7 constant_dynamic-slice_fusion
  221.9 2.0 collective-permute-start.12
  226.1 12.8 %collective-permute-done.12 = bf16[128,2048]{1,0:T(8,128)(2,1)} collective-permute-done((bf16[128,2048]{1,0:T(8,128)(2,1)}, bf16[128,2048]{1,0:T(8,128)(2,1)}, u32[]{:S(2)}, u32[]{:S(2)}) %collective-permute-start.12) | collective-permute-done | bytes 524320 | tf_op jit(solution)/shard_map/ppermute | solution.py:32
  241.7 18.9 %collective-permute-done.25 = bf16[128,2048]{1,0:T(8,128)(2,1)} collective-permute-done((bf16[128,2048]{1,0:T(8,128)(2,1)}, bf16[128,2048]{1,0:T(8,128)(2,1)}, u32[]{:S(2)}, u32[]{:S(2)}) %collective-permute-start.25) | collective-permute-done | bytes 524320 | tf_op jit(solution)/shard_map/ppermute | solution.py:32
  260.7 1.8 fusion
  263.9 2.8 add_convert_fusion.3
  266.7 1.5 collective-permute-start.30
  268.3 9.3 %collective-permute-done.27 = bf16[128,2048]{1,0:T(8,128)(2,1)S(1)} collective-permute-done((bf16[128,2048]{1,0:T(8,128)(2,1)}, bf16[128,2048]{1,0:T(8,128)(2,1)S(1)}, u32[]{:S(2)}, u32[]{:S(2)}) %collective-permute-start.27) | collective-permute-done | bytes 524320 | tf_op jit(solution)/shard_map/ppermute | solution.py:32
  277.6 1.5 collective-permute-start.33
  279.1 2.7 add_convert_fusion.4
  281.7 17.7 %collective-permute-done.13 = bf16[128,2048]{1,0:T(8,128)(2,1)S(1)} collective-permute-done((bf16[128,2048]{1,0:T(8,128)(2,1)S(1)}, bf16[128,2048]{1,0:T(8,128)(2,1)S(1)}, u32[]{:S(2)}, u32[]{:S(2)}) %collective-permute-start.13) | collective-permute-done | bytes 524320 | tf_op jit(solution)/shard_map/ppermute | solution.py:32
  299.4 2.3 add_convert_fusion.8
  301.8 1.7 fusion.2
  304.8 9.6 %collective-permute-done.33 = bf16[8,128,512]{2,1,0:T(8,128)(2,1)} collective-permute-done((bf16[8,128,512]{2,1,0:T(8,128)(2,1)}, bf16[8,128,512]{2,1,0:T(8,128)(2,1)}, u32[]{:S(2)}, u32[]{:S(2)}) %collective-permute-start.33) | collective-permute-done | bytes 1048608 | tf_op jit(solution)/shard_map/ppermute | solution.py:32
  314.3 3.3 %add_convert_fusion.2 = bf16[8,128,512]{2,1,0:T(8,128)(2,1)} fusion(bf16[8,128,512]{2,1,0:T(8,128)(2,1)} %collective-permute-done.33, bf16[8,128,512]{2,1,0:T(8,128)(2,1)} %collective-permute-done.31, bf16[8,128,2048]{2,1,0:T(8,128)(2,1)} %copy-done, s32[]{:T(128)S(6)} %select_n.70), kind=kLoop, calls=%fused_computation.21 | loop fusion | flops 3145728 | bytes 4194308 | tf_op jit(solution)/shard_map/convert_element_type | solution.py:139
  (88 shorter events, 26.5 us)
Async XLA Ops:
  0.6 55.9 %copy-start.4 = (bf16[128,2048]{1,0:T(8,128)(2,1)S(1)}, bf16[128,2048]{1,0:T(8,128)(2,1)}, u32[]{:S(2)}) copy-start(bf16[128,2048]{1,0:T(8,128)(2,1)} %param.9) | copy-start | bytes 1572868
  3.8 18.1 %collective-permute-start.3 = (bf16[128,2176]{0,1:T(8,128)(2,1)S(1)}, bf16[128,2176]{0,1:T(8,128)(2,1)S(1)}, u32[]{:S(2)}, u32[]{:S(2)}) collective-permute-start(bf16[128,2176]{0,1:T(8,128)(2,1)S(1)} %pad_maximum_fusion.1), channel_id=1, source_target_pairs={{0,24},{4,28},{8,0},{12,4},{16,8},{20,12},{24,16},{28,20},{1,25},{... | collective-permute-start | bytes 1671176 | tf_op jit(solution)/shard_map/ppermute | solution.py:32
  8.9 26.0 %collective-permute-start = (bf16[128,2176]{0,1:T(8,128)(2,1)S(1)}, bf16[128,2176]{0,1:T(8,128)(2,1)S(1)}, u32[]{:S(2)}, u32[]{:S(2)}) collective-permute-start(bf16[128,2176]{0,1:T(8,128)(2,1)S(1)} %pad_maximum_fusion.1), channel_id=1, source_target_pairs={{0,8},{4,12},{8,16},{12,20},{16,24},{20,28},{24,0},{28,4},{1,9},{5... | collective-permute-start | bytes 1671176 | tf_op jit(solution)/shard_map/ppermute | solution.py:32
  8.9 47.6 %collective-permute-start.1 = (bf16[128,2176]{0,1:T(8,128)(2,1)S(1)}, bf16[128,2176]{0,1:T(8,128)(2,1)S(1)}, u32[]{:S(2)}, u32[]{:S(2)}) collective-permute-start(bf16[128,2176]{0,1:T(8,128)(2,1)S(1)} %pad_maximum_fusion.1), channel_id=1, source_target_pairs={{0,16},{4,20},{8,24},{12,28},{16,0},{20,4},{24,8},{28,12},{1,17},{... | collective-permute-start | bytes 1671176 | tf_op jit(solution)/shard_map/ppermute | solution.py:32
  9.9 49.2 %collective-permute-start.5 = (bf16[128,2176]{0,1:T(8,128)(2,1)S(1)}, bf16[128,2176]{0,1:T(8,128)(2,1)}, u32[]{:S(2)}, u32[]{:S(2)}) collective-permute-start(bf16[128,2176]{0,1:T(8,128)(2,1)S(1)} %pad_maximum_fusion.1), channel_id=1, source_target_pairs={{0,4},{4,0},{8,12},{12,8},{16,20},{20,16},{24,28},{28,24},{1,5},{5... | collective-permute-start | bytes 1671176 | tf_op jit(solution)/shard_map/ppermute | solution.py:32
  21.9 82.2 %collective-permute-start.4 = (bf16[128,2176]{0,1:T(8,128)(2,1)S(1)}, bf16[128,2176]{0,1:T(8,128)(2,1)}, u32[]{:S(2)}, u32[]{:S(2)}) collective-permute-start(bf16[128,2176]{0,1:T(8,128)(2,1)S(1)} %collective-permute-done.3), channel_id=1, source_target_pairs={{0,4},{4,0},{8,12},{12,8},{16,20},{20,16},{24,28},{28,24},{1,5},{5... | collective-permute-start | bytes 1671176 | tf_op jit(solution)/shard_map/ppermute | solution.py:32
  34.9 70.8 %collective-permute-start.2 = (bf16[128,2176]{0,1:T(8,128)(2,1)S(1)}, bf16[128,2176]{0,1:T(8,128)(2,1)}, u32[]{:S(2)}, u32[]{:S(2)}) collective-permute-start(bf16[128,2176]{0,1:T(8,128)(2,1)S(1)} %collective-permute-done), channel_id=1, source_target_pairs={{0,4},{4,0},{8,12},{12,8},{16,20},{20,16},{24,28},{28,24},{1,5},{5... | collective-permute-start | bytes 1671176 | tf_op jit(solution)/shard_map/ppermute | solution.py:32
  56.5 15.0 %collective-permute-start.17 = (bf16[128,2048]{1,0:T(8,128)(2,1)S(1)}, bf16[128,2048]{1,0:T(8,128)(2,1)}, u32[]{:S(2)}, u32[]{:S(2)}) collective-permute-start(bf16[128,2048]{1,0:T(8,128)(2,1)S(1)} %copy-done.4), channel_id=1, source_target_pairs={{0,24},{4,28},{8,0},{12,4},{16,8},{20,12},{24,16},{28,20},{1,25},{... | collective-permute-start | bytes 1572872 | tf_op jit(solution)/shard_map/ppermute | solution.py:32
  59.1 43.0 %collective-permute-start.15 = (bf16[128,2048]{1,0:T(8,128)(2,1)S(1)}, bf16[128,2048]{1,0:T(8,128)(2,1)}, u32[]{:S(2)}, u32[]{:S(2)}) collective-permute-start(bf16[128,2048]{1,0:T(8,128)(2,1)S(1)} %copy-done.4), channel_id=1, source_target_pairs={{0,16},{4,20},{8,24},{12,28},{16,0},{20,4},{24,8},{28,12},{1,17},{... | collective-permute-start | bytes 1572872 | tf_op jit(solution)/shard_map/ppermute | solution.py:32
  59.2 44.4 %collective-permute-start.14 = (bf16[128,2048]{1,0:T(8,128)(2,1)S(1)}, bf16[128,2048]{1,0:T(8,128)(2,1)}, u32[]{:S(2)}, u32[]{:S(2)}) collective-permute-start(bf16[128,2048]{1,0:T(8,128)(2,1)S(1)} %copy-done.4), channel_id=1, source_target_pairs={{0,8},{4,12},{8,16},{12,20},{16,24},{20,28},{24,0},{28,4},{1,9},{5... | collective-permute-start | bytes 1572872 | tf_op jit(solution)/shard_map/ppermute | solution.py:32
  71.5 81.3 %collective-permute-start.19 = (bf16[128,2048]{1,0:T(8,128)(2,1)S(1)}, bf16[128,2048]{1,0:T(8,128)(2,1)S(1)}, u32[]{:S(2)}, u32[]{:S(2)}) collective-permute-start(bf16[128,2048]{1,0:T(8,128)(2,1)S(1)} %copy-done.4), channel_id=1, source_target_pairs={{0,4},{4,0},{8,12},{12,8},{16,20},{20,16},{24,28},{28,24},{1,5},{5... | collective-permute-start | bytes 1572872 | tf_op jit(solution)/shard_map/ppermute | solution.py:32
  102.1 15.5 %collective-permute-start.6 = (bf16[128,2176]{0,1:T(8,128)(2,1)S(1)}, bf16[128,2176]{0,1:T(8,128)(2,1)S(1)}, u32[]{:S(2)}, u32[]{:S(2)}) collective-permute-start(bf16[128,2176]{0,1:T(8,128)(2,1)S(1)} %collective-permute-done.1), channel_id=1, source_target_pairs={{0,4},{4,0},{8,12},{12,8},{16,20},{20,16},{24,28},{28,24},{1,5},{5... | collective-permute-start | bytes 1671176 | tf_op jit(solution)/shard_map/ppermute | solution.py:32
  103.6 32.0 %collective-permute-start.18 = (bf16[128,2048]{1,0:T(8,128)(2,1)}, bf16[128,2048]{1,0:T(8,128)(2,1)S(1)}, u32[]{:S(2)}, u32[]{:S(2)}) collective-permute-start(bf16[128,2048]{1,0:T(8,128)(2,1)} %collective-permute-done.17), channel_id=1, source_target_pairs={{0,4},{4,0},{8,12},{12,8},{16,20},{20,16},{24,28},{28,24},{1,5},{5... | collective-permute-start | bytes 1572872 | tf_op jit(solution)/shard_map/ppermute | solution.py:32
  104.1 48.7 %collective-permute-start.20 = (bf16[128,2048]{1,0:T(8,128)(2,1)}, bf16[128,2048]{1,0:T(8,128)(2,1)S(1)}, u32[]{:S(2)}, u32[]{:S(2)}) collective-permute-start(bf16[128,2048]{1,0:T(8,128)(2,1)} %collective-permute-done.15), channel_id=1, source_target_pairs={{0,4},{4,0},{8,12},{12,8},{16,20},{20,16},{24,28},{28,24},{1,5},{5... | collective-permute-start | bytes 1572872 | tf_op jit(solution)/shard_map/ppermute | solution.py:32
  105.6 45.7 %collective-permute-start.16 = (bf16[128,2048]{1,0:T(8,128)(2,1)}, bf16[128,2048]{1,0:T(8,128)(2,1)S(1)}, u32[]{:S(2)}, u32[]{:S(2)}) collective-permute-start(bf16[128,2048]{1,0:T(8,128)(2,1)} %collective-permute-done.14), channel_id=1, source_target_pairs={{0,4},{4,0},{8,12},{12,8},{16,20},{20,16},{24,28},{28,24},{1,5},{5... | collective-permute-start | bytes 1572872 | tf_op jit(solution)/shard_map/ppermute | solution.py:32
  109.1 10.0 %copy-start.1 = (bf16[512,2176]{0,1:T(8,128)(2,1)}, bf16[512,2176]{0,1:T(8,128)(2,1)S(1)}, u32[]{:S(2)}) copy-start(bf16[512,2176]{0,1:T(8,128)(2,1)S(1)} %pad_maximum_fusion) | copy-start | bytes 6684676
  119.0 2.2 copy-start.10
  125.2 2.9 copy-start.9
  131.6 35.4 %collective-permute-start.10 = (bf16[128,2048]{1,0:T(8,128)(2,1)S(1)}, bf16[128,2048]{1,0:T(8,128)(2,1)S(1)}, u32[]{:S(2)}, u32[]{:S(2)}) collective-permute-start(bf16[128,2048]{1,0:T(8,128)(2,1)S(1)} %get-tuple-element.59), channel_id=1, source_target_pairs={{0,4},{4,0},{8,12},{12,8},{16,20},{20,16},{24,28},{28,24},{1,5},{5... | collective-permute-start | bytes 1572872 | tf_op jit(solution)/shard_map/ppermute | solution.py:32
  135.7 62.3 %collective-permute-start.9 = (bf16[128,2048]{1,0:T(8,128)(2,1)S(1)}, bf16[128,2048]{1,0:T(8,128)(2,1)S(1)}, u32[]{:S(2)}, u32[]{:S(2)}) collective-permute-start(bf16[128,2048]{1,0:T(8,128)(2,1)S(1)} %get-tuple-element.60), channel_id=1, source_target_pairs={{0,4},{4,0},{8,12},{12,8},{16,20},{20,16},{24,28},{28,24},{1,5},{5... | collective-permute-start | bytes 1572872 | tf_op jit(solution)/shard_map/ppermute | solution.py:32
  151.3 74.0 %collective-permute-start.8 = (bf16[128,2048]{1,0:T(8,128)(2,1)S(1)}, bf16[128,2048]{1,0:T(8,128)(2,1)S(1)}, u32[]{:S(2)}, u32[]{:S(2)}) collective-permute-start(bf16[128,2048]{1,0:T(8,128)(2,1)S(1)} %get-tuple-element.61), channel_id=1, source_target_pairs={{0,4},{4,0},{8,12},{12,8},{16,20},{20,16},{24,28},{28,24},{1,5},{5... | collective-permute-start | bytes 1572872 | tf_op jit(solution)/shard_map/ppermute | solution.py:32
  160.0 1.8 copy-start.11
  161.0 35.3 %collective-permute-start.23 = (bf16[128,2048]{1,0:T(8,128)(2,1)S(1)}, bf16[128,2048]{1,0:T(8,128)(2,1)S(1)}, u32[]{:S(2)}, u32[]{:S(2)}) collective-permute-start(bf16[128,2048]{1,0:T(8,128)(2,1)S(1)} %get-tuple-element.54), channel_id=1, source_target_pairs={{0,4},{4,0},{8,12},{12,8},{16,20},{20,16},{24,28},{28,24},{1,5},{5... | collective-permute-start | bytes 1572872 | tf_op jit(solution)/shard_map/ppermute | solution.py:32
  167.2 30.7 %collective-permute-start.11 = (bf16[128,2048]{1,0:T(8,128)(2,1)S(1)}, bf16[128,2048]{1,0:T(8,128)(2,1)S(1)}, u32[]{:S(2)}, u32[]{:S(2)}) collective-permute-start(bf16[128,2048]{1,0:T(8,128)(2,1)S(1)} %add_convert_fusion.11), channel_id=1, source_target_pairs={{0,24},{4,28},{8,0},{12,4},{16,8},{20,12},{24,16},{28,20},{1,25},{... | collective-permute-start | bytes 1572872 | tf_op jit(solution)/shard_map/ppermute | solution.py:32
  169.6 54.3 %copy-start.3 = (bf16[512,2048]{1,0:T(8,128)(2,1)}, bf16[512,2048]{1,0:T(8,128)(2,1)S(1)}, u32[]{:S(2)}) copy-start(bf16[512,2048]{1,0:T(8,128)(2,1)S(1)} %bitcast_convert_fusion.1) | copy-start | bytes 6291460
  169.6 51.8 %collective-permute-start.26 = (bf16[128,2048]{1,0:T(8,128)(2,1)S(1)}, bf16[128,2048]{1,0:T(8,128)(2,1)S(1)}, u32[]{:S(2)}, u32[]{:S(2)}) collective-permute-start(bf16[128,2048]{1,0:T(8,128)(2,1)S(1)} %get-tuple-element.53), channel_id=1, source_target_pairs={{0,4},{4,0},{8,12},{12,8},{16,20},{20,16},{24,28},{28,24},{1,5},{5... | collective-permute-start | bytes 1572872 | tf_op jit(solution)/shard_map/ppermute | solution.py:32
  196.3 27.7 %collective-permute-start.22 = (bf16[128,2048]{1,0:T(8,128)(2,1)S(1)}, bf16[128,2048]{1,0:T(8,128)(2,1)S(1)}, u32[]{:S(2)}, u32[]{:S(2)}) collective-permute-start(bf16[128,2048]{1,0:T(8,128)(2,1)S(1)} %get-tuple-element.55), channel_id=1, source_target_pairs={{0,4},{4,0},{8,12},{12,8},{16,20},{20,16},{24,28},{28,24},{1,5},{5... | collective-permute-start | bytes 1572872 | tf_op jit(solution)/shard_map/ppermute | solution.py:32
  197.9 5.8 %slice-start = ((bf16[512,2176]{0,1:T(8,128)(2,1)}), bf16[512,2048]{0,1:T(8,128)(2,1)S(1)}, s32[]{:S(2)}) async-start(bf16[512,2176]{0,1:T(8,128)(2,1)} %copy-done.1), calls=%async_computation | async-start | bytes 4194304 | tf_op jit(solution)/shard_map/slice | solution.py:158
  197.9 24.0 %collective-permute-start.24 = (bf16[128,2048]{1,0:T(8,128)(2,1)S(1)}, bf16[128,2048]{1,0:T(8,128)(2,1)S(1)}, u32[]{:S(2)}, u32[]{:S(2)}) collective-permute-start(bf16[128,2048]{1,0:T(8,128)(2,1)S(1)} %add_convert_fusion.7), channel_id=1, source_target_pairs={{0,24},{4,28},{8,0},{12,4},{16,8},{20,12},{24,16},{28,20},{1,25},{... | collective-permute-start | bytes 1572872 | tf_op jit(solution)/shard_map/ppermute | solution.py:32
  209.5 2.6 copy-start.2
  212.0 48.6 %collective-permute-start.29 = (bf16[8,512,128]{1,2,0:T(8,128)(2,1)}, bf16[8,512,128]{1,2,0:T(8,128)(2,1)}, u32[]{:S(2)}, u32[]{:S(2)}) collective-permute-start(bf16[8,512,128]{1,2,0:T(8,128)(2,1)} %get-tuple-element.51), channel_id=1, source_target_pairs={{0,1},{1,0},{2,3},{3,2},{4,5},{5,4},{6,7},{7,6},{8,9},{9,8},{10,11... | collective-permute-start | bytes 3145736 | tf_op jit(solution)/shard_map/ppermute | solution.py:32
  218.6 2.8 copy-start
  221.4 20.2 %collective-permute-start.21 = (bf16[128,2048]{1,0:T(8,128)(2,1)}, bf16[128,2048]{1,0:T(8,128)(2,1)}, u32[]{:S(2)}, u32[]{:S(2)}) collective-permute-start(bf16[128,2048]{1,0:T(8,128)(2,1)} %get-tuple-element.52), channel_id=1, source_target_pairs={{0,4},{4,0},{8,12},{12,8},{16,20},{20,16},{24,28},{28,24},{1,5},{5... | collective-permute-start | bytes 1572872 | tf_op jit(solution)/shard_map/ppermute | solution.py:32
  221.9 3.4 %copy-start.6 = (bf16[128,2048]{1,0:T(8,128)(2,1)}, bf16[128,2048]{1,0:T(8,128)(2,1)S(1)}, u32[]{:S(2)}) copy-start(bf16[128,2048]{1,0:T(8,128)(2,1)S(1)} %collective-permute-done.24) | copy-start | bytes 1572868
  221.9 17.0 %collective-permute-start.12 = (bf16[128,2048]{1,0:T(8,128)(2,1)}, bf16[128,2048]{1,0:T(8,128)(2,1)}, u32[]{:S(2)}, u32[]{:S(2)}) collective-permute-start(bf16[128,2048]{1,0:T(8,128)(2,1)} %add_convert_fusion.10), channel_id=1, source_target_pairs={{0,8},{4,12},{8,16},{12,20},{16,24},{20,28},{24,0},{28,4},{1,9},{5... | collective-permute-start | bytes 1572872 | tf_op jit(solution)/shard_map/ppermute | solution.py:32
  223.9 38.6 %collective-permute-start.32 = (bf16[8,128,512]{2,1,0:T(8,128)(2,1)}, bf16[8,128,512]{2,1,0:T(8,128)(2,1)}, u32[]{:S(2)}, u32[]{:S(2)}) collective-permute-start(bf16[8,128,512]{2,1,0:T(8,128)(2,1)} %get-tuple-element.49), channel_id=1, source_target_pairs={{0,1},{1,0},{2,3},{3,2},{4,5},{5,4},{6,7},{7,6},{8,9},{9,8},{10,11... | collective-permute-start | bytes 3145736 | tf_op jit(solution)/shard_map/ppermute | solution.py:32
  225.3 0.8 copy-start.8
  226.1 34.5 %collective-permute-start.25 = (bf16[128,2048]{1,0:T(8,128)(2,1)}, bf16[128,2048]{1,0:T(8,128)(2,1)}, u32[]{:S(2)}, u32[]{:S(2)}) collective-permute-start(bf16[128,2048]{1,0:T(8,128)(2,1)} %get-tuple-element.57), channel_id=1, source_target_pairs={{0,16},{4,20},{8,24},{12,28},{16,0},{20,4},{24,8},{28,12},{1,17},{... | collective-permute-start | bytes 1572872 | tf_op jit(solution)/shard_map/ppermute | solution.py:32
  239.0 27.8 %collective-permute-start.7 = (bf16[128,2048]{1,0:T(8,128)(2,1)}, bf16[128,2048]{1,0:T(8,128)(2,1)S(1)}, u32[]{:S(2)}, u32[]{:S(2)}) collective-permute-start(bf16[128,2048]{1,0:T(8,128)(2,1)} %get-tuple-element.58), channel_id=1, source_target_pairs={{0,4},{4,0},{8,12},{12,8},{16,20},{20,16},{24,28},{28,24},{1,5},{5... | collective-permute-start | bytes 1572872 | tf_op jit(solution)/shard_map/ppermute | solution.py:32
  241.6 60.1 %collective-permute-start.28 = (bf16[8,512,128]{1,2,0:T(8,128)(2,1)}, bf16[8,512,128]{1,2,0:T(8,128)(2,1)S(1)}, u32[]{:S(2)}, u32[]{:S(2)}) collective-permute-start(bf16[8,512,128]{1,2,0:T(8,128)(2,1)} %get-tuple-element.50), channel_id=1, source_target_pairs={{0,1},{1,0},{2,3},{3,2},{4,5},{5,4},{6,7},{7,6},{8,9},{9,8},{10,11... | collective-permute-start | bytes 3145736 | tf_op jit(solution)/shard_map/ppermute | solution.py:32
  260.6 44.2 %collective-permute-start.31 = (bf16[8,128,512]{2,1,0:T(8,128)(2,1)}, bf16[8,128,512]{2,1,0:T(8,128)(2,1)}, u32[]{:S(2)}, u32[]{:S(2)}) collective-permute-start(bf16[8,128,512]{2,1,0:T(8,128)(2,1)} %get-tuple-element.48), channel_id=1, source_target_pairs={{0,1},{1,0},{2,3},{3,2},{4,5},{5,4},{6,7},{7,6},{8,9},{9,8},{10,11... | collective-permute-start | bytes 3145736 | tf_op jit(solution)/shard_map/ppermute | solution.py:32
  260.7 16.9 %collective-permute-start.27 = (bf16[128,2048]{1,0:T(8,128)(2,1)}, bf16[128,2048]{1,0:T(8,128)(2,1)S(1)}, u32[]{:S(2)}, u32[]{:S(2)}) collective-permute-start(bf16[128,2048]{1,0:T(8,128)(2,1)} %get-tuple-element.56), channel_id=1, source_target_pairs={{0,8},{4,12},{8,16},{12,20},{16,24},{20,28},{24,0},{28,4},{1,9},{5... | collective-permute-start | bytes 1572872 | tf_op jit(solution)/shard_map/ppermute | solution.py:32
  262.5 16.6 %copy-start.7 = (bf16[128,2048]{1,0:T(8,128)(2,1)S(1)}, bf16[128,2048]{1,0:T(8,128)(2,1)}, u32[]{:S(2)}) copy-start(bf16[128,2048]{1,0:T(8,128)(2,1)} %copy-done.6) | copy-start | bytes 1572868
  262.5 36.9 %collective-permute-start.13 = (bf16[128,2048]{1,0:T(8,128)(2,1)S(1)}, bf16[128,2048]{1,0:T(8,128)(2,1)S(1)}, u32[]{:S(2)}, u32[]{:S(2)}) collective-permute-start(bf16[128,2048]{1,0:T(8,128)(2,1)S(1)} %add_convert_fusion.9), channel_id=1, source_target_pairs={{0,16},{4,20},{8,24},{12,28},{16,0},{20,4},{24,8},{28,12},{1,17},{... | collective-permute-start | bytes 1572872 | tf_op jit(solution)/shard_map/ppermute | solution.py:32
  266.7 32.7 %copy-start.5 = (bf16[128,2048]{1,0:T(8,128)(2,1)S(1)}, bf16[128,2048]{1,0:T(8,128)(2,1)}, u32[]{:S(2)}) copy-start(bf16[128,2048]{1,0:T(8,128)(2,1)} %param.6) | copy-start | bytes 1572868
  266.7 35.0 %collective-permute-start.30 = (bf16[8,512,128]{1,2,0:T(8,128)(2,1)S(1)}, bf16[8,512,128]{1,2,0:T(8,128)(2,1)S(1)}, u32[]{:S(2)}, u32[]{:S(2)}) collective-permute-start(bf16[8,512,128]{1,2,0:T(8,128)(2,1)S(1)} %fusion), channel_id=1, source_target_pairs={{0,2},{1,3},{2,0},{3,1},{4,6},{5,7},{6,4},{7,5},{8,10},{9,11},{10,... | collective-permute-start | bytes 3145736 | tf_op jit(solution)/shard_map/ppermute | solution.py:32
  277.6 36.8 %collective-permute-start.33 = (bf16[8,128,512]{2,1,0:T(8,128)(2,1)}, bf16[8,128,512]{2,1,0:T(8,128)(2,1)}, u32[]{:S(2)}, u32[]{:S(2)}) collective-permute-start(bf16[8,128,512]{2,1,0:T(8,128)(2,1)} %add_convert_fusion.3), channel_id=1, source_target_pairs={{0,2},{1,3},{2,0},{3,1},{4,6},{5,7},{6,4},{7,5},{8,10},{9,11},{10,... | collective-permute-start | bytes 3145736 | tf_op jit(solution)/shard_map/ppermute | solution.py:32
